TPU v7x, 256 devices: a whole 4x4x8 slice. The times are simulated.
256 devices in a mesh: seq: 16 (over z, core), head: 16 (over x, y).
Axes of the slice: x: 4, y: 4, z: 8, core: 2. Of those that a mesh axis runs over, the one named last changes fastest.
Arguments:
- queries: bfloat16 [4096, 16384], P('seq', 'head'), may hold values from -8 to 8
- keys: bfloat16 [4096, 1024], P('seq'), may hold values from -8 to 8
- values: bfloat16 [4096, 1024], P('seq'), may hold values from -8 to 8
- query_map: bfloat16 [128, 128, 128], P('head'), may hold values from -3 to 3
- key_map: bfloat16 [8, 128, 128], replicated, may hold values from -3 to 3
- positions: int32 [4096], P('seq'), may hold values from 0 to 131071, as said below
Outputs:
- error_grad: bfloat16 [4096, 16384], P('seq', 'head')
Inputs may be any that keep to these rules, and one draw needn't show every extreme that they name: `positions`: each token's position is one more than the token before it, or 0 where a new document begins; the window begins inside a document that ends at position 131071, and at least one document begins inside the window.
All inputs are finite; a program needn't handle non-finite values.
Results may differ from a plain program's by a relative error of at most 0.0085.
Values may be sent and summed in bfloat16 or wider, within the bound.
No kernel may reach another device: no remote copies, remote signals or barrier semaphores. Data moves between devices by JAX's collectives and lax.ppermute only.
A program may use at most 64 MiB of HBM per device.

v0:
```python
import math

import jax
import jax.numpy as jnp
from jax import lax
from jax.experimental import pallas as pl
from jax.experimental.pallas import tpu as pltpu
from jax.sharding import Mesh
from jax.sharding import PartitionSpec as P


QHEADS = 128
KVH = 8
LENGTH = 131072
HD = 128
ROWS = 272
TOK = 256
epsilon = 1e-06
masked_score = -1e30
to_exp2 = math.log2(math.e) / math.sqrt(HD)

SWAP = [(0, 1), (1, 0)]


def ring(shift):
    return [(i, (i + shift) % 8) for i in range(8)]


def call(kernel, out_shape, in_specs=None, scratch=(), flops=0, nbytes=0,
         aliases=None):
    more = {} if in_specs is None else {"in_specs": in_specs}
    return pl.pallas_call(
        kernel,
        out_shape=out_shape,
        **more,
        input_output_aliases=aliases or {},
        scratch_shapes=list(scratch),
        compiler_params=pltpu.CompilerParams(vmem_limit_bytes=40 * 1024 * 1024),
        cost_estimate=pl.CostEstimate(
            flops=flops, bytes_accessed=nbytes, transcendentals=0
        ),
    )


def first_group(local_heads):
    return lax.axis_index("head") * local_heads // (QHEADS // KVH)


def pieces(x):
    a = x.astype(jnp.bfloat16)
    x = x - a.astype(jnp.float32)
    b = x.astype(jnp.bfloat16)
    c = (x - b.astype(jnp.float32)).astype(jnp.bfloat16)
    return a.astype(jnp.float32), b.astype(jnp.float32), c.astype(jnp.float32)


def pack_kernel(keys_ref, values_ref, pos_ref, out_ref, pos_vmem, sems):
    g = pl.multiple_of(first_group(8) * HD, HD)
    cp = pltpu.make_async_copy(pos_ref, pos_vmem, sems.at[2])
    ck = pltpu.make_async_copy(keys_ref.at[:, pl.ds(g, HD)], out_ref.at[0:TOK, 0:HD], sems.at[0])
    cv = pltpu.make_async_copy(
        values_ref.at[:, pl.ds(g, HD)], out_ref.at[0:TOK, HD : 2 * HD], sems.at[1]
    )
    cp.start()
    ck.start()
    cv.start()
    cp.wait()
    a = (0.5 * math.pi / LENGTH) * pos_vmem[...].astype(jnp.float32)
    row = lax.broadcasted_iota(jnp.int32, (16, TOK), 0)
    tile = jnp.zeros((16, TOK), jnp.float32)
    for i, part in enumerate(pieces(jnp.cos(a)) + pieces(jnp.sin(a))):
        tile = jnp.where(row == i, part, tile)
    out_ref[TOK:ROWS, :] = tile.astype(jnp.bfloat16)
    ck.wait()
    cv.wait()


def angles_of(block_ref):
    d = block_ref[TOK:ROWS, :].astype(jnp.float32)
    return d[0:1] + d[1:2] + d[2:3], d[3:4] + d[4:5] + d[5:6]


def elu1(x):
    return jnp.where(x > 0.0, x + 1.0, jnp.exp(jnp.minimum(x, 0.0)))


def dot(a, b, dims):
    return lax.dot_general(a, b, (dims, ((), ())), preferred_element_type=jnp.float32)


def nn(a, b):
    return dot(a, b, ((1,), (0,)))


def nt(a, b):
    return dot(a, b, ((1,), (1,)))


def key_feats_t(block_ref, key_map, ok=None):
    c, s = angles_of(block_ref)
    if ok is not None:
        c, s = jnp.where(ok, c, 0.0), jnp.where(ok, s, 0.0)
    phi = elu1(dot(key_map, block_ref[0:TOK, 0:HD], ((0,), (1,))))
    return jnp.concatenate([c * phi, s * phi], axis=0).astype(jnp.bfloat16)


def with_ones(v):
    return jnp.concatenate([v, jnp.ones(v.shape, v.dtype)], axis=1)


def local_kernel(own_ref, q_ref, qmap_ref, kmap_ref, qf_ref, m_ref, accl_ref, stu_ref):
    k = own_ref[0:TOK, 0:HD]
    va = with_ones(own_ref[0:TOK, HD : 2 * HD])
    c, s = angles_of(own_ref)
    ct = jnp.broadcast_to(c, (HD, TOK)).T
    st = jnp.broadcast_to(s, (HD, TOK)).T
    kft = key_feats_t(own_ref, kmap_ref[first_group(8)])
    causal = lax.broadcasted_iota(jnp.int32, (TOK, TOK), 0) >= lax.broadcasted_iota(
        jnp.int32, (TOK, TOK), 1
    )
    for h in range(8):
        q = q_ref[:, h * HD : (h + 1) * HD]
        phi = elu1(nn(q, qmap_ref[h]))
        qf = jnp.concatenate([ct * phi, st * phi], axis=1).astype(jnp.bfloat16)
        qf_ref[h] = qf
        inner = jnp.where(causal, nn(qf, kft), 0.0).astype(jnp.bfloat16)
        stu_ref[h] = nn(inner, va)
        x = jnp.where(causal, nt(q, k), masked_score)
        m = jnp.max(x, axis=1, keepdims=True)
        p = jnp.exp2((x - m) * to_exp2).astype(jnp.bfloat16)
        accl_ref[h] = nn(p, va)
        m_ref[h] = jnp.broadcast_to(m, (TOK, HD))


def scores_of(q_ref, h, blocks):
    q = q_ref[:, h * HD : (h + 1) * HD]
    return [nt(q, b[0:TOK, 0:HD]) for b, _ in blocks]


def softmax_step(xs, blocks, va, m0, accl):
    top = None
    for x, (_, ok) in zip(xs, blocks):
        t = jnp.where(ok, jnp.maximum(x[:, 0:HD], x[:, HD:]), masked_score)
        top = t if top is None else jnp.maximum(top, t)
    top = jnp.max(top, axis=1, keepdims=True)
    m1 = jnp.maximum(m0, jnp.broadcast_to(top, m0.shape))
    f = jnp.exp2((m0 - m1) * to_exp2)
    ps = []
    for x, (_, ok) in zip(xs, blocks):
        mm = jnp.where(ok, m1, -masked_score)
        p = jnp.exp2((x - jnp.concatenate([mm, mm], axis=1)) * to_exp2)
        ps.append(p.astype(jnp.bfloat16))
    add = nn(jnp.concatenate(ps, axis=1), va)
    return m1, accl * jnp.concatenate([f, f], axis=1) + add


def values_of(blocks):
    return jnp.concatenate([with_ones(b[0:TOK, HD : 2 * HD]) for b, _ in blocks], axis=0)


def absorb(blocks, q_ref, kmap_ref, m_from, accl_from, state, m_ref, accl_ref):
    km = kmap_ref[first_group(8)]
    va = values_of(blocks)
    feats = [None] * len(blocks)
    later = scores_of(q_ref, 0, blocks)
    for h in range(8):
        xs = later
        if h < 7:
            later = scores_of(q_ref, h + 1, blocks)
        for i in range(h, len(blocks), 8):
            feats[i] = key_feats_t(blocks[i][0], km, blocks[i][1])
        m_ref[h], accl_ref[h] = softmax_step(xs, blocks, va, m_from[h], accl_from[h])
    return state + nn(jnp.concatenate(feats, axis=1), va)


def near_kernel(pb, u1, u1s, d1, d1s, q_ref, kmap_ref, m_in, accl_in, m_ref, accl_ref, state_ref):
    z = lax.axis_index("z")
    second = lax.axis_index("c") == 1
    ins = (q_ref, kmap_ref, m_in, accl_in)
    outs = (m_ref, accl_ref)

    @pl.when(z == 0)
    def _():
        state_ref[...] = absorb([(pb, second)], *ins, 0.0, *outs)

    @pl.when(z >= 1)
    def _():
        blocks = [(pb, second), (u1, z >= 1), (u1s, z >= 1)]
        state_ref[...] = absorb(blocks, *ins, 0.0, *outs)

    @pl.when(z >= 7)
    def _():
        blocks = [(d1, z >= 7), (d1s, z >= 7)]
        state_ref[...] = absorb(blocks, q_ref, kmap_ref, m_ref, accl_ref, state_ref[...], *outs)


def mid_kernel(x, xs, u2, u2s, d2, d2s, q_ref, kmap_ref, m_in, accl_in, state_in,
               m_ref, accl_ref, state_ref):
    z = lax.axis_index("z")
    blocks = [(u2, z >= 2), (u2s, z >= 2), (x, z >= 4), (xs, z >= 4)]

    @pl.when((z >= 2) & (z < 6))
    def _():
        state_ref[...] = absorb(
            blocks, q_ref, kmap_ref, m_in, accl_in, state_in[...], m_ref, accl_ref
        )

    @pl.when(z >= 6)
    def _():
        state_ref[...] = absorb(
            blocks + [(d2, z >= 6), (d2s, z >= 6)],
            q_ref, kmap_ref, m_in, accl_in, state_in[...], m_ref, accl_ref,
        )


def edge_kernel(u3, d3, q_ref, kmap_ref, m_in, accl_in, state_in, m_ref, accl_ref, state_ref):
    z = lax.axis_index("z")
    ins = (q_ref, kmap_ref, m_in, accl_in)

    @pl.when((z >= 3) & (z < 5))
    def _():
        state_ref[...] = absorb([(u3, z >= 3)], *ins, state_in[...], m_ref, accl_ref)

    @pl.when(z >= 5)
    def _():
        blocks = [(u3, z >= 3), (d3, z >= 5)]
        state_ref[...] = absorb(blocks, *ins, state_in[...], m_ref, accl_ref)


def last_kernel(u3s, d3s, q_ref, kmap_ref, qf_ref, stu_ref, m_in, accl_in, state_in,
                out_ref):
    z = lax.axis_index("z")

    def finish(blocks):
        state = state_in[...]
        if blocks:
            km = kmap_ref[first_group(8)]
            va = values_of(blocks)
            feats = [key_feats_t(b, km, ok) for b, ok in blocks]
            later = scores_of(q_ref, 0, blocks)
            state = state + nn(jnp.concatenate(feats, axis=1), va)
        high = state.astype(jnp.bfloat16)
        for h in range(8):
            accl = accl_in[h]
            if blocks:
                xs = later
                if h < 7:
                    later = scores_of(q_ref, h + 1, blocks)
                _, accl = softmax_step(xs, blocks, va, m_in[h], accl)
            qf = qf_ref[h]
            nd = stu_ref[h] + nn(qf, high)
            student = nd[:, 0:HD] / (nd[:, HD:] + epsilon)
            teacher = (accl[:, 0:HD] / accl[:, HD:]).astype(jnp.bfloat16).astype(jnp.float32)
            out_ref[:, h * HD : (h + 1) * HD] = (2.0 * (student - teacher)).astype(jnp.bfloat16)

    near = [(u3s, z >= 3)]

    @pl.when(z >= 5)
    def _():
        finish(near + [(d3s, z >= 5)])

    @pl.when((z >= 3) & (z < 5))
    def _():
        finish(near)

    @pl.when(z < 3)
    def _():
        finish([])


def per_device(queries, keys, values, query_map, key_map, positions):
    f32, bf16 = jnp.float32, jnp.bfloat16
    any_ = pl.BlockSpec(memory_space=pltpu.HBM)
    vm = pl.BlockSpec(memory_space=pltpu.VMEM)
    own = pl.pallas_call(
        pack_kernel,
        out_shape=jax.ShapeDtypeStruct((ROWS, 2 * HD), bf16),
        in_specs=[any_, any_, any_],
        out_specs=vm,
        scratch_shapes=[pltpu.VMEM((1, TOK), jnp.int32), pltpu.SemaphoreType.DMA((3,))],
        name="pack",
        cost_estimate=pl.CostEstimate(flops=4 << 30, bytes_accessed=16 << 20, transcendentals=0),
    )(keys, values, positions.reshape(1, TOK))

    def swap(a):
        return lax.ppermute(a, "c", SWAP)

    def hop(a, shift):
        return lax.ppermute(a, "z", ring(shift))

    u1 = hop(own, 1)
    d1 = hop(own, -1)
    x4 = hop(own, 4)
    u2 = hop(u1, 1)
    d2 = hop(d1, -1)
    u3 = hop(u2, 1)
    d3 = hop(d2, -1)

    heads = lambda w, t: jax.ShapeDtypeStruct((8, TOK, w), t)
    state = jax.ShapeDtypeStruct((2 * HD, 2 * HD), f32)
    qf, m, accl, stu = call(
        local_kernel,
        (
            heads(256, bf16),
            heads(HD, f32),
            heads(256, f32),
            heads(256, f32),
        ),
        flops=8 * 2 * 256 * 128 * 1500,
        nbytes=8 << 20,
    )(own, queries, query_map, key_map)
    m, accl, st = call(
        near_kernel,
        (heads(HD, f32), heads(256, f32), state),
        flops=8 * 2 * 256 * 128 * 3000,
        nbytes=8 << 20,
        aliases={7: 0, 8: 1},
    )(swap(own), u1, swap(u1), d1, swap(d1), queries, key_map, m, accl)
    m, accl, st = call(
        mid_kernel,
        (heads(HD, f32), heads(256, f32), state),
        flops=8 * 2 * 256 * 128 * 4000,
        nbytes=8 << 20,
        aliases={8: 0, 9: 1, 10: 2},
    )(x4, swap(x4), u2, swap(u2), d2, swap(d2), queries, key_map, m,
      accl, st)
    m, accl, st = call(
        edge_kernel,
        (heads(HD, f32), heads(256, f32), state),
        flops=8 * 2 * 256 * 128 * 1500,
        nbytes=8 << 20,
        aliases={4: 0, 5: 1, 6: 2},
    )(u3, d3, queries, key_map, m, accl, st)
    return call(
        last_kernel,
        jax.ShapeDtypeStruct((TOK, 8 * HD), bf16),
        flops=8 * 2 * 256 * 128 * 3000,
        nbytes=8 << 20,
    )(swap(u3), swap(d3), queries, key_map, qf, stu, m, accl, st)


def solution(mesh):
    split = Mesh(mesh.devices.reshape(8, 2, mesh.shape["head"]), ("z", "c", "head"))
    seq = ("z", "c")
    placed = (P(seq, "head"), P(seq, None), P(seq, None), P("head", None, None), P(), P(seq))
    return jax.shard_map(
        per_device, mesh=split, in_specs=placed, out_specs=P(seq, "head"), check_vma=False
    )
```

profile of v0, /device:TPU:101, one launch (start us, length us, event | category | flops | bytes accessed | tf_op | source)
XLA Modules:
  0.0 41.2 jit_solution(1858569410529246055)
XLA Ops:
  0.0 0.0 copy-start
  0.0 0.0 copy-start.1
  0.0 0.0 copy-start.2
  0.0 1.7 %pack.1.own_ref = bf16[272,256]{1,0:T(8,128)(2,1)} custom-call(bf16[256,1024]{1,0:T(8,128)(2,1)} %keys_ref.1, bf16[256,1024]{1,0:T(8,128)(2,1)} %values_ref.1, s32[1,256]{1,0:T(1,128)} %bitcast.1), custom_call_target="tpu_custom_call" | custom-call | flops 4294967296 | bytes 16777216 | tf_op jit(solution)/shard_map/pack/pallas_call | solution.py:275
  1.7 2.9 %collective-permute-start = (bf16[272,256]{1,0:T(8,128)(2,1)}, bf16[272,256]{1,0:T(8,128)(2,1)S(1)}, u32[]{:S(2)}, u32[]{:S(2)}) collective-permute-start(bf16[272,256]{1,0:T(8,128)(2,1)} %pack.1.own_ref), channel_id=1, source_target_pairs={{0,32},{32,64},{64,96},{96,128},{128,160},{160,192},{192,224},{224... | collective-permute-start | bytes 417800 | tf_op jit(solution)/shard_map/ppermute | solution.py:289
  4.6 0.0 collective-permute-start.4
  4.6 1.0 %collective-permute-start.12 = (bf16[272,256]{1,0:T(8,128)(2,1)}, bf16[272,256]{1,0:T(8,128)(2,1)S(1)}, u32[]{:S(2)}, u32[]{:S(2)}) collective-permute-start(bf16[272,256]{1,0:T(8,128)(2,1)} %pack.1.own_ref), channel_id=1, source_target_pairs={{0,16},{16,0},{1,17},{17,1},{2,18},{18,2},{3,19},{19,3},{4,20},{20... | collective-permute-start | bytes 417800 | tf_op jit(solution)/shard_map/ppermute | solution.py:286
  5.6 3.1 %collective-permute-start.8 = (bf16[272,256]{1,0:T(8,128)(2,1)}, bf16[272,256]{1,0:T(8,128)(2,1)S(1)}, u32[]{:S(2)}, u32[]{:S(2)}) collective-permute-start(bf16[272,256]{1,0:T(8,128)(2,1)} %pack.1.own_ref), channel_id=1, source_target_pairs={{0,128},{32,160},{64,192},{96,224},{128,0},{160,32},{192,64},{224,... | collective-permute-start | bytes 417800 | tf_op jit(solution)/shard_map/ppermute | solution.py:289
  8.7 0.0 collective-permute-done.u1
  8.7 1.9 %collective-permute-start.1 = (bf16[272,256]{1,0:T(8,128)(2,1)S(1)}, bf16[272,256]{1,0:T(8,128)(2,1)S(1)}, u32[]{:S(2)}, u32[]{:S(2)}) collective-permute-start(bf16[272,256]{1,0:T(8,128)(2,1)S(1)} %collective-permute-done.u1), channel_id=1, source_target_pairs={{0,32},{32,64},{64,96},{96,128},{128,160},{160,192},{192,224},{224... | collective-permute-start | bytes 417800 | tf_op jit(solution)/shard_map/ppermute | solution.py:289
  10.6 1.8 %collective-permute-start.13 = (bf16[272,256]{1,0:T(8,128)(2,1)S(1)}, bf16[272,256]{1,0:T(8,128)(2,1)S(1)}, u32[]{:S(2)}, u32[]{:S(2)}) collective-permute-start(bf16[272,256]{1,0:T(8,128)(2,1)S(1)} %collective-permute-done.u1), channel_id=1, source_target_pairs={{0,16},{16,0},{1,17},{17,1},{2,18},{18,2},{3,19},{19,3},{4,20},{20... | collective-permute-start | bytes 417800 | tf_op jit(solution)/shard_map/ppermute | solution.py:286
  12.4 0.0 collective-permute-done.4.d1
  12.4 0.0 collective-permute-start.5
  12.4 0.0 collective-permute-done.12.pb
  12.4 4.6 %collective-permute-start.14 = (bf16[272,256]{1,0:T(8,128)(2,1)S(1)}, bf16[272,256]{1,0:T(8,128)(2,1)S(1)}, u32[]{:S(2)}, u32[]{:S(2)}) collective-permute-start(bf16[272,256]{1,0:T(8,128)(2,1)S(1)} %collective-permute-done.4.d1), channel_id=1, source_target_pairs={{0,16},{16,0},{1,17},{17,1},{2,18},{18,2},{3,19},{19,3},{4,20},{20... | collective-permute-start | bytes 417800 | tf_op jit(solution)/shard_map/ppermute | solution.py:286
  17.0 0.0 copy-done
  17.0 0.0 copy-done.1
  17.0 0.0 copy-done.2
  17.0 0.0 copy-start.3
  17.0 0.9 %copy-done.3 = bf16[272,256]{1,0:T(8,128)(2,1)S(1)} copy-done((bf16[272,256]{1,0:T(8,128)(2,1)S(1)}, bf16[272,256]{1,0:T(8,128)(2,1)}, u32[]{:S(2)}) %copy-start.3) | copy-done | bytes 139288
  17.9 3.2 %shard_map.64 = (bf16[8,256,256]{2,1,0:T(8,128)(2,1)S(1)}, f32[8,256,128]{2,1,0:T(8,128)S(1)}, f32[8,256,256]{2,1,0:T(8,128)S(1)}, f32[8,256,256]{2,1,0:T(8,128)S(1)}) custom-call(bf16[272,256]{1,0:T(8,128)(2,1)S(1)} %copy-done.3, bf16[256,1024]{1,0:T(8,128)(2,1)S(1)} %copy-done, bf16[8,128,128]{2,1,0:T(8,128)(2,1)S(1)} %copy-done.2, ...), custom_call_target="tpu_custom_call" | custom-call | flops 786432000 | bytes 8388608 | tf_op jit(solution)/shard_map/pallas_call | solution.py:301
  21.2 0.0 collective-permute-done.8.x
  21.2 0.1 collective-permute-start.9
  21.3 0.0 collective-permute-done.1.u2
  21.3 0.5 %collective-permute-start.10 = (bf16[272,256]{1,0:T(8,128)(2,1)S(1)}, bf16[272,256]{1,0:T(8,128)(2,1)S(1)}, u32[]{:S(2)}, u32[]{:S(2)}) collective-permute-start(bf16[272,256]{1,0:T(8,128)(2,1)S(1)} %collective-permute-done.1.u2), channel_id=1, source_target_pairs={{0,16},{16,0},{1,17},{17,1},{2,18},{18,2},{3,19},{19,3},{4,20},{20... | collective-permute-start | bytes 417800 | tf_op jit(solution)/shard_map/ppermute | solution.py:286
  21.8 0.0 collective-permute-done.13.u1s
  21.8 3.0 %collective-permute-start.2 = (bf16[272,256]{1,0:T(8,128)(2,1)S(1)}, bf16[272,256]{1,0:T(8,128)(2,1)S(1)}, u32[]{:S(2)}, u32[]{:S(2)}) collective-permute-start(bf16[272,256]{1,0:T(8,128)(2,1)S(1)} %collective-permute-done.1.u2), channel_id=1, source_target_pairs={{0,32},{32,64},{64,96},{96,128},{128,160},{160,192},{192,224},{224... | collective-permute-start | bytes 417800 | tf_op jit(solution)/shard_map/ppermute | solution.py:289
  24.7 0.0 collective-permute-done.5.d2
  24.7 0.4 collective-permute-start.11
  25.1 0.0 collective-permute-done.14.d1s
  25.1 0.0 collective-permute-start.6
  25.1 2.9 %shard_map.65 = (f32[8,256,128]{2,1,0:T(8,128)S(1)}, f32[8,256,256]{2,1,0:T(8,128)S(1)}, f32[256,256]{1,0:T(8,128)S(1)}) custom-call(bf16[272,256]{1,0:T(8,128)(2,1)S(1)} %collective-permute-done.12.pb, bf16[272,256]{1,0:T(8,128)(2,1)S(1)} %collective-permute-done.u1, ...), custom_call_target="tpu_custom_call", output_to_operand_aliasing={{0}: (7, {}), {1}: (8, {})} | custom-call | flops 1572864000 | bytes 8388608 | tf_op jit(solution)/shard_map/pallas_call | solution.py:312
  28.1 0.0 collective-permute-done.2.u3
  28.1 0.5 %collective-permute-start.3 = (bf16[272,256]{1,0:T(8,128)(2,1)S(1)}, bf16[272,256]{1,0:T(8,128)(2,1)S(1)}, u32[]{:S(2)}, u32[]{:S(2)}) collective-permute-start(bf16[272,256]{1,0:T(8,128)(2,1)S(1)} %collective-permute-done.2.u3), channel_id=1, source_target_pairs={{0,16},{16,0},{1,17},{17,1},{2,18},{18,2},{3,19},{19,3},{4,20},{20... | collective-permute-start | bytes 417800 | tf_op jit(solution)/shard_map/ppermute | solution.py:286
  28.6 2.8 %collective-permute-done.6.d3 = bf16[272,256]{1,0:T(8,128)(2,1)S(1)} collective-permute-done((bf16[272,256]{1,0:T(8,128)(2,1)S(1)}, bf16[272,256]{1,0:T(8,128)(2,1)S(1)}, u32[]{:S(2)}, u32[]{:S(2)}) %collective-permute-start.6) | collective-permute-done | bytes 139296 | tf_op jit(solution)/shard_map/ppermute | solution.py:289
  31.5 1.0 %collective-permute-start.7 = (bf16[272,256]{1,0:T(8,128)(2,1)S(1)}, bf16[272,256]{1,0:T(8,128)(2,1)S(1)}, u32[]{:S(2)}, u32[]{:S(2)}) collective-permute-start(bf16[272,256]{1,0:T(8,128)(2,1)S(1)} %collective-permute-done.6.d3), channel_id=1, source_target_pairs={{0,16},{16,0},{1,17},{17,1},{2,18},{18,2},{3,19},{19,3},{4,20},{20... | collective-permute-start | bytes 417800 | tf_op jit(solution)/shard_map/ppermute | solution.py:286
  32.4 0.0 collective-permute-done.9.xs
  32.4 0.0 collective-permute-done.10.u2s
  32.4 0.0 collective-permute-done.11.d2s
  32.4 4.4 %shard_map.66 = (f32[8,256,128]{2,1,0:T(8,128)S(1)}, f32[8,256,256]{2,1,0:T(8,128)S(1)}, f32[256,256]{1,0:T(8,128)S(1)}) custom-call(bf16[272,256]{1,0:T(8,128)(2,1)S(1)} %collective-permute-done.8.x, bf16[272,256]{1,0:T(8,128)(2,1)S(1)} %collective-permute-done.9.xs, ...), custom_call_target="tpu_custom_call", output_to_operand_aliasing={{0}: (8, {}), {1}: (9, {}), {2}: (10, {})} | custom-call | flops 2097152000 | bytes 8388608 | tf_op jit(solution)/shard_map/pallas_call | solution.py:319
  36.9 1.8 %shard_map.67 = (f32[8,256,128]{2,1,0:T(8,128)S(1)}, f32[8,256,256]{2,1,0:T(8,128)S(1)}, f32[256,256]{1,0:T(8,128)S(1)}) custom-call(bf16[272,256]{1,0:T(8,128)(2,1)S(1)} %collective-permute-done.2.u3, bf16[272,256]{1,0:T(8,128)(2,1)S(1)} %collective-permute-done.6.d3, ...), custom_call_target="tpu_custom_call", output_to_operand_aliasing={{0}: (4, {}), {1}: (5, {}), {2}: (6, {})} | custom-call | flops 786432000 | bytes 8388608 | tf_op jit(solution)/shard_map/pallas_call | solution.py:327
  38.7 0.0 collective-permute-done.3.u3s
  38.7 0.0 collective-permute-done.7.d3s
  38.7 2.4 %shard_map.68 = bf16[256,1024]{1,0:T(8,128)(2,1)} custom-call(bf16[272,256]{1,0:T(8,128)(2,1)S(1)} %collective-permute-done.3.u3s, bf16[272,256]{1,0:T(8,128)(2,1)S(1)} %collective-permute-done.7.d3s, bf16[256,1024]{1,0:T(8,128)(2,1)S(1)} %copy-done, bf16[8,128,128]{2,1,0:T(8,128)(2,1)S(1)} %copy-done.1, bf16[8,256,256]{2,1,0:T(8,128)(2,1)S(1)} %get-tuple-element.18.qf_ref, ...), custom_call_target="tpu_custom_call" | custom-call | flops 1572864000 | bytes 8388608 | tf_op jit(solution)/shard_map/pallas_call | solution.py:334
Async XLA Ops:
  0.0 17.0 %copy-start = (bf16[256,1024]{1,0:T(8,128)(2,1)S(1)}, bf16[256,1024]{1,0:T(8,128)(2,1)}, u32[]{:S(2)}) copy-start(bf16[256,1024]{1,0:T(8,128)(2,1)} %q_ref.9) | copy-start | bytes 1572868
  0.0 17.0 %copy-start.1 = (bf16[8,128,128]{2,1,0:T(8,128)(2,1)S(1)}, bf16[8,128,128]{2,1,0:T(8,128)(2,1)}, u32[]{:S(2)}) copy-start(bf16[8,128,128]{2,1,0:T(8,128)(2,1)} %kmap_ref.9) | copy-start | bytes 786436
  0.0 17.0 %copy-start.2 = (bf16[8,128,128]{2,1,0:T(8,128)(2,1)S(1)}, bf16[8,128,128]{2,1,0:T(8,128)(2,1)}, u32[]{:S(2)}) copy-start(bf16[8,128,128]{2,1,0:T(8,128)(2,1)} %qmap_ref.1) | copy-start | bytes 786436
  1.7 7.0 %collective-permute-start = (bf16[272,256]{1,0:T(8,128)(2,1)}, bf16[272,256]{1,0:T(8,128)(2,1)S(1)}, u32[]{:S(2)}, u32[]{:S(2)}) collective-permute-start(bf16[272,256]{1,0:T(8,128)(2,1)} %pack.1.own_ref), channel_id=1, source_target_pairs={{0,32},{32,64},{64,96},{96,128},{128,160},{160,192},{192,224},{224... | collective-permute-start | bytes 417800 | tf_op jit(solution)/shard_map/ppermute | solution.py:289
  4.6 7.8 %collective-permute-start.4 = (bf16[272,256]{1,0:T(8,128)(2,1)}, bf16[272,256]{1,0:T(8,128)(2,1)S(1)}, u32[]{:S(2)}, u32[]{:S(2)}) collective-permute-start(bf16[272,256]{1,0:T(8,128)(2,1)} %pack.1.own_ref), channel_id=1, source_target_pairs={{0,224},{32,0},{64,32},{96,64},{128,96},{160,128},{192,160},{224,1... | collective-permute-start | bytes 417800 | tf_op jit(solution)/shard_map/ppermute | solution.py:289
  4.6 7.8 %collective-permute-start.12 = (bf16[272,256]{1,0:T(8,128)(2,1)}, bf16[272,256]{1,0:T(8,128)(2,1)S(1)}, u32[]{:S(2)}, u32[]{:S(2)}) collective-permute-start(bf16[272,256]{1,0:T(8,128)(2,1)} %pack.1.own_ref), channel_id=1, source_target_pairs={{0,16},{16,0},{1,17},{17,1},{2,18},{18,2},{3,19},{19,3},{4,20},{20... | collective-permute-start | bytes 417800 | tf_op jit(solution)/shard_map/ppermute | solution.py:286
  5.6 15.6 %collective-permute-start.8 = (bf16[272,256]{1,0:T(8,128)(2,1)}, bf16[272,256]{1,0:T(8,128)(2,1)S(1)}, u32[]{:S(2)}, u32[]{:S(2)}) collective-permute-start(bf16[272,256]{1,0:T(8,128)(2,1)} %pack.1.own_ref), channel_id=1, source_target_pairs={{0,128},{32,160},{64,192},{96,224},{128,0},{160,32},{192,64},{224,... | collective-permute-start | bytes 417800 | tf_op jit(solution)/shard_map/ppermute | solution.py:289
  8.7 12.6 %collective-permute-start.1 = (bf16[272,256]{1,0:T(8,128)(2,1)S(1)}, bf16[272,256]{1,0:T(8,128)(2,1)S(1)}, u32[]{:S(2)}, u32[]{:S(2)}) collective-permute-start(bf16[272,256]{1,0:T(8,128)(2,1)S(1)} %collective-permute-done.u1), channel_id=1, source_target_pairs={{0,32},{32,64},{64,96},{96,128},{128,160},{160,192},{192,224},{224... | collective-permute-start | bytes 417800 | tf_op jit(solution)/shard_map/ppermute | solution.py:289
  10.6 11.2 %collective-permute-start.13 = (bf16[272,256]{1,0:T(8,128)(2,1)S(1)}, bf16[272,256]{1,0:T(8,128)(2,1)S(1)}, u32[]{:S(2)}, u32[]{:S(2)}) collective-permute-start(bf16[272,256]{1,0:T(8,128)(2,1)S(1)} %collective-permute-done.u1), channel_id=1, source_target_pairs={{0,16},{16,0},{1,17},{17,1},{2,18},{18,2},{3,19},{19,3},{4,20},{20... | collective-permute-start | bytes 417800 | tf_op jit(solution)/shard_map/ppermute | solution.py:286
  12.4 12.3 %collective-permute-start.5 = (bf16[272,256]{1,0:T(8,128)(2,1)S(1)}, bf16[272,256]{1,0:T(8,128)(2,1)S(1)}, u32[]{:S(2)}, u32[]{:S(2)}) collective-permute-start(bf16[272,256]{1,0:T(8,128)(2,1)S(1)} %collective-permute-done.4.d1), channel_id=1, source_target_pairs={{0,224},{32,0},{64,32},{96,64},{128,96},{160,128},{192,160},{224,1... | collective-permute-start | bytes 417800 | tf_op jit(solution)/shard_map/ppermute | solution.py:289
  12.4 12.7 %collective-permute-start.14 = (bf16[272,256]{1,0:T(8,128)(2,1)S(1)}, bf16[272,256]{1,0:T(8,128)(2,1)S(1)}, u32[]{:S(2)}, u32[]{:S(2)}) collective-permute-start(bf16[272,256]{1,0:T(8,128)(2,1)S(1)} %collective-permute-done.4.d1), channel_id=1, source_target_pairs={{0,16},{16,0},{1,17},{17,1},{2,18},{18,2},{3,19},{19,3},{4,20},{20... | collective-permute-start | bytes 417800 | tf_op jit(solution)/shard_map/ppermute | solution.py:286
  17.0 0.9 %copy-start.3 = (bf16[272,256]{1,0:T(8,128)(2,1)S(1)}, bf16[272,256]{1,0:T(8,128)(2,1)}, u32[]{:S(2)}) copy-start(bf16[272,256]{1,0:T(8,128)(2,1)} %pack.1.own_ref) | copy-start | bytes 417796
  21.2 11.3 %collective-permute-start.9 = (bf16[272,256]{1,0:T(8,128)(2,1)S(1)}, bf16[272,256]{1,0:T(8,128)(2,1)S(1)}, u32[]{:S(2)}, u32[]{:S(2)}) collective-permute-start(bf16[272,256]{1,0:T(8,128)(2,1)S(1)} %collective-permute-done.8.x), channel_id=1, source_target_pairs={{0,16},{16,0},{1,17},{17,1},{2,18},{18,2},{3,19},{19,3},{4,20},{20... | collective-permute-start | bytes 417800 | tf_op jit(solution)/shard_map/ppermute | solution.py:286
  21.3 11.1 %collective-permute-start.10 = (bf16[272,256]{1,0:T(8,128)(2,1)S(1)}, bf16[272,256]{1,0:T(8,128)(2,1)S(1)}, u32[]{:S(2)}, u32[]{:S(2)}) collective-permute-start(bf16[272,256]{1,0:T(8,128)(2,1)S(1)} %collective-permute-done.1.u2), channel_id=1, source_target_pairs={{0,16},{16,0},{1,17},{17,1},{2,18},{18,2},{3,19},{19,3},{4,20},{20... | collective-permute-start | bytes 417800 | tf_op jit(solution)/shard_map/ppermute | solution.py:286
  21.8 6.3 %collective-permute-start.2 = (bf16[272,256]{1,0:T(8,128)(2,1)S(1)}, bf16[272,256]{1,0:T(8,128)(2,1)S(1)}, u32[]{:S(2)}, u32[]{:S(2)}) collective-permute-start(bf16[272,256]{1,0:T(8,128)(2,1)S(1)} %collective-permute-done.1.u2), channel_id=1, source_target_pairs={{0,32},{32,64},{64,96},{96,128},{128,160},{160,192},{192,224},{224... | collective-permute-start | bytes 417800 | tf_op jit(solution)/shard_map/ppermute | solution.py:289
  24.7 7.7 %collective-permute-start.11 = (bf16[272,256]{1,0:T(8,128)(2,1)S(1)}, bf16[272,256]{1,0:T(8,128)(2,1)S(1)}, u32[]{:S(2)}, u32[]{:S(2)}) collective-permute-start(bf16[272,256]{1,0:T(8,128)(2,1)S(1)} %collective-permute-done.5.d2), channel_id=1, source_target_pairs={{0,16},{16,0},{1,17},{17,1},{2,18},{18,2},{3,19},{19,3},{4,20},{20... | collective-permute-start | bytes 417800 | tf_op jit(solution)/shard_map/ppermute | solution.py:286
  25.1 6.3 %collective-permute-start.6 = (bf16[272,256]{1,0:T(8,128)(2,1)S(1)}, bf16[272,256]{1,0:T(8,128)(2,1)S(1)}, u32[]{:S(2)}, u32[]{:S(2)}) collective-permute-start(bf16[272,256]{1,0:T(8,128)(2,1)S(1)} %collective-permute-done.5.d2), channel_id=1, source_target_pairs={{0,224},{32,0},{64,32},{96,64},{128,96},{160,128},{192,160},{224,1... | collective-permute-start | bytes 417800 | tf_op jit(solution)/shard_map/ppermute | solution.py:289
  28.1 10.6 %collective-permute-start.3 = (bf16[272,256]{1,0:T(8,128)(2,1)S(1)}, bf16[272,256]{1,0:T(8,128)(2,1)S(1)}, u32[]{:S(2)}, u32[]{:S(2)}) collective-permute-start(bf16[272,256]{1,0:T(8,128)(2,1)S(1)} %collective-permute-done.2.u3), channel_id=1, source_target_pairs={{0,16},{16,0},{1,17},{17,1},{2,18},{18,2},{3,19},{19,3},{4,20},{20... | collective-permute-start | bytes 417800 | tf_op jit(solution)/shard_map/ppermute | solution.py:286
  31.5 7.3 %collective-permute-start.7 = (bf16[272,256]{1,0:T(8,128)(2,1)S(1)}, bf16[272,256]{1,0:T(8,128)(2,1)S(1)}, u32[]{:S(2)}, u32[]{:S(2)}) collective-permute-start(bf16[272,256]{1,0:T(8,128)(2,1)S(1)} %collective-permute-done.6.d3), channel_id=1, source_target_pairs={{0,16},{16,0},{1,17},{17,1},{2,18},{18,2},{3,19},{19,3},{4,20},{20... | collective-permute-start | bytes 417800 | tf_op jit(solution)/shard_map/ppermute | solution.py:286
where the time goes:
time: 41.3 us; the launch traced here: 41.2 us
  starting transfers between devices  20.8 us (50%)
  Pallas kernels  16.5 us (40%)
  waiting for transfers between devices  2.86 us (7%)
  local copies, waits for them, and re-layouts  0.91 us (2%)
    ppermute x7, starting transfers between devices, hop(): return lax.ppermute(a, 'z', ring(shift))  10.9 us
    ppermute x8, starting transfers between devices, swap(): return lax.ppermute(a, 'c', SWAP)  9.89 us
    pallas_call x1, Pallas kernels, per_device(): call(mid_kernel, (heads(HD, f32), heads(256, f32), state), flops=8 * 2 *...  4.45 us
    pallas_call x1, Pallas kernels, per_device(): call(local_kernel, (heads(256, bf16), heads(HD, f32), heads(256, f32), he...  3.21 us
    pallas_call x1, Pallas kernels, per_device(): call(near_kernel, (heads(HD, f32), heads(256, f32), state), flops=8 * 2 *...  2.94 us
    ppermute x7, waiting for transfers between devices, hop(): return lax.ppermute(a, 'z', ring(shift))  2.84 us
    pallas_call x1, Pallas kernels, per_device(): call(last_kernel, jax.ShapeDtypeStruct((TOK, 8 * HD), bf16), flops=8 * 2...  2.44 us
    pallas_call x1, Pallas kernels, per_device(): call(edge_kernel, (heads(HD, f32), heads(256, f32), state), flops=8 * 2 *...  1.79 us
  transfers between devices with their start and end apart: 15, of which 1 were waited for; matrix products, arithmetic and copies ran while one was open for 0% of the time, Pallas kernels for 30%

commit v1 on v0

--- a/solution.py
+++ b/solution.py
@@ -173,7 +173,7 @@
     return state + nn(jnp.concatenate(feats, axis=1), va)
 
 
-def near_kernel(pb, u1, u1s, d1, d1s, q_ref, kmap_ref, m_in, accl_in, m_ref, accl_ref, state_ref):
+def near_kernel(pb, u1, u1s, q_ref, kmap_ref, m_in, accl_in, m_ref, accl_ref, state_ref):
     z = lax.axis_index("z")
     second = lax.axis_index("c") == 1
     ins = (q_ref, kmap_ref, m_in, accl_in)
@@ -188,16 +188,22 @@
         blocks = [(pb, second), (u1, z >= 1), (u1s, z >= 1)]
         state_ref[...] = absorb(blocks, *ins, 0.0, *outs)
 
+
+def wrap_kernel(d1, d1s, q_ref, kmap_ref, m_in, accl_in, state_in, m_ref, accl_ref, state_ref):
+    z = lax.axis_index("z")
+
     @pl.when(z >= 7)
     def _():
         blocks = [(d1, z >= 7), (d1s, z >= 7)]
-        state_ref[...] = absorb(blocks, q_ref, kmap_ref, m_ref, accl_ref, state_ref[...], *outs)
-
-
-def mid_kernel(x, xs, u2, u2s, d2, d2s, q_ref, kmap_ref, m_in, accl_in, state_in,
+        state_ref[...] = absorb(
+            blocks, q_ref, kmap_ref, m_in, accl_in, state_in[...], m_ref, accl_ref
+        )
+
+
+def mid_kernel(u2, u2s, d2, d2s, q_ref, kmap_ref, m_in, accl_in, state_in,
                m_ref, accl_ref, state_ref):
     z = lax.axis_index("z")
-    blocks = [(u2, z >= 2), (u2s, z >= 2), (x, z >= 4), (xs, z >= 4)]
+    blocks = [(u2, z >= 2), (u2s, z >= 2)]
 
     @pl.when((z >= 2) & (z < 6))
     def _():
@@ -213,21 +219,18 @@
         )
 
 
-def edge_kernel(u3, d3, q_ref, kmap_ref, m_in, accl_in, state_in, m_ref, accl_ref, state_ref):
-    z = lax.axis_index("z")
-    ins = (q_ref, kmap_ref, m_in, accl_in)
-
-    @pl.when((z >= 3) & (z < 5))
-    def _():
-        state_ref[...] = absorb([(u3, z >= 3)], *ins, state_in[...], m_ref, accl_ref)
-
-    @pl.when(z >= 5)
-    def _():
-        blocks = [(u3, z >= 3), (d3, z >= 5)]
-        state_ref[...] = absorb(blocks, *ins, state_in[...], m_ref, accl_ref)
-
-
-def last_kernel(u3s, d3s, q_ref, kmap_ref, qf_ref, stu_ref, m_in, accl_in, state_in,
+def far_kernel(x, xs, q_ref, kmap_ref, m_in, accl_in, state_in, m_ref, accl_ref, state_ref):
+    z = lax.axis_index("z")
+
+    @pl.when(z >= 4)
+    def _():
+        state_ref[...] = absorb(
+            [(x, z >= 4), (xs, z >= 4)],
+            q_ref, kmap_ref, m_in, accl_in, state_in[...], m_ref, accl_ref,
+        )
+
+
+def last_kernel(u3, u3s, d3, d3s, q_ref, kmap_ref, qf_ref, stu_ref, m_in, accl_in, state_in,
                 out_ref):
     z = lax.axis_index("z")
 
@@ -253,11 +256,11 @@
             teacher = (accl[:, 0:HD] / accl[:, HD:]).astype(jnp.bfloat16).astype(jnp.float32)
             out_ref[:, h * HD : (h + 1) * HD] = (2.0 * (student - teacher)).astype(jnp.bfloat16)
 
-    near = [(u3s, z >= 3)]
+    near = [(u3, z >= 3), (u3s, z >= 3)]
 
     @pl.when(z >= 5)
     def _():
-        finish(near + [(d3s, z >= 5)])
+        finish(near + [(d3, z >= 5), (d3s, z >= 5)])
 
     @pl.when((z >= 3) & (z < 5))
     def _():
@@ -314,29 +317,35 @@
         (heads(HD, f32), heads(256, f32), state),
         flops=8 * 2 * 256 * 128 * 3000,
         nbytes=8 << 20,
-        aliases={7: 0, 8: 1},
-    )(swap(own), u1, swap(u1), d1, swap(d1), queries, key_map, m, accl)
+        aliases={5: 0, 6: 1},
+    )(swap(own), u1, swap(u1), queries, key_map, m, accl)
+    m, accl, st = call(
+        wrap_kernel,
+        (heads(HD, f32), heads(256, f32), state),
+        flops=8 * 2 * 256 * 128 * 1000,
+        nbytes=8 << 20,
+        aliases={4: 0, 5: 1, 6: 2},
+    )(d1, swap(d1), queries, key_map, m, accl, st)
     m, accl, st = call(
         mid_kernel,
         (heads(HD, f32), heads(256, f32), state),
-        flops=8 * 2 * 256 * 128 * 4000,
-        nbytes=8 << 20,
-        aliases={8: 0, 9: 1, 10: 2},
-    )(x4, swap(x4), u2, swap(u2), d2, swap(d2), queries, key_map, m,
-      accl, st)
+        flops=8 * 2 * 256 * 128 * 3000,
+        nbytes=8 << 20,
+        aliases={6: 0, 7: 1, 8: 2},
+    )(u2, swap(u2), d2, swap(d2), queries, key_map, m, accl, st)
     m, accl, st = call(
-        edge_kernel,
+        far_kernel,
         (heads(HD, f32), heads(256, f32), state),
         flops=8 * 2 * 256 * 128 * 1500,
         nbytes=8 << 20,
         aliases={4: 0, 5: 1, 6: 2},
-    )(u3, d3, queries, key_map, m, accl, st)
+    )(x4, swap(x4), queries, key_map, m, accl, st)
     return call(
         last_kernel,
         jax.ShapeDtypeStruct((TOK, 8 * HD), bf16),
         flops=8 * 2 * 256 * 128 * 3000,
         nbytes=8 << 20,
-    )(swap(u3), swap(d3), queries, key_map, qf, stu, m, accl, st)
+    )(u3, swap(u3), d3, swap(d3), queries, key_map, qf, stu, m, accl, st)
 
 
 def solution(mesh):

time: 41.3 us -> 41.3 us (level)
  the two profiles are of different devices: /device:TPU:101 before, /device:TPU:237 now
where the time goes in v1:
time: 41.3 us; the launch traced here: 41.2 us
  Pallas kernels  21.2 us (51%)
  starting transfers between devices  16.6 us (40%)
  waiting for transfers between devices  2.32 us (6%)
  local copies, waits for them, and re-layouts  0.91 us (2%)
    ppermute x7, starting transfers between devices, hop(): return lax.ppermute(a, 'z', ring(shift))  10.6 us
    ppermute x8, starting transfers between devices, swap(): return lax.ppermute(a, 'c', SWAP)  5.99 us
    pallas_call x1, Pallas kernels, per_device(): call(last_kernel, jax.ShapeDtypeStruct((TOK, 8 * HD), bf16), flops=8 * 2...  4.71 us
    pallas_call x1, Pallas kernels, per_device(): call(mid_kernel, (heads(HD, f32), heads(256, f32), state), flops=8 * 2 *...  3.81 us
    pallas_call x1, Pallas kernels, per_device(): call(local_kernel, (heads(256, bf16), heads(HD, f32), heads(256, f32), he...  3.17 us
    pallas_call x1, Pallas kernels, per_device(): call(near_kernel, (heads(HD, f32), heads(256, f32), state), flops=8 * 2 *...  3 us
    pallas_call x1, Pallas kernels, per_device(): call(wrap_kernel, (heads(HD, f32), heads(256, f32), state), flops=8 * 2 *...  2.43 us
    pallas_call x1, Pallas kernels, per_device(): call(far_kernel, (heads(HD, f32), heads(256, f32), state), flops=8 * 2 *...  2.41 us
  transfers between devices with their start and end apart: 15, of which 2 were waited for; matrix products, arithmetic and copies ran while one was open for 0% of the time, Pallas kernels for 36%

profile of v1, /device:TPU:237, one launch (start us, length us, event | category | flops | bytes accessed | tf_op | source)
XLA Modules:
  0.0 41.2 jit_solution(1616544262805225972)
XLA Ops:
  0.0 0.0 copy-start
  0.0 0.0 copy-start.1
  0.0 0.0 copy-start.2
  0.0 1.7 %pack.1.own_ref = bf16[272,256]{1,0:T(8,128)(2,1)} custom-call(bf16[256,1024]{1,0:T(8,128)(2,1)} %keys_ref.1, bf16[256,1024]{1,0:T(8,128)(2,1)} %values_ref.1, s32[1,256]{1,0:T(1,128)} %bitcast.1), custom_call_target="tpu_custom_call" | custom-call | flops 4294967296 | bytes 16777216 | tf_op jit(solution)/shard_map/pack/pallas_call | solution.py:278
  1.7 0.1 collective-permute-start
  1.8 1.5 %collective-permute-start.4 = (bf16[272,256]{1,0:T(8,128)(2,1)}, bf16[272,256]{1,0:T(8,128)(2,1)S(1)}, u32[]{:S(2)}, u32[]{:S(2)}) collective-permute-start(bf16[272,256]{1,0:T(8,128)(2,1)} %pack.1.own_ref), channel_id=1, source_target_pairs={{0,224},{32,0},{64,32},{96,64},{128,96},{160,128},{192,160},{224,1... | collective-permute-start | bytes 417800 | tf_op jit(solution)/shard_map/ppermute | solution.py:292
  3.2 1.2 %collective-permute-start.13 = (bf16[272,256]{1,0:T(8,128)(2,1)}, bf16[272,256]{1,0:T(8,128)(2,1)S(1)}, u32[]{:S(2)}, u32[]{:S(2)}) collective-permute-start(bf16[272,256]{1,0:T(8,128)(2,1)} %pack.1.own_ref), channel_id=1, source_target_pairs={{0,16},{16,0},{1,17},{17,1},{2,18},{18,2},{3,19},{19,3},{4,20},{20... | collective-permute-start | bytes 417800 | tf_op jit(solution)/shard_map/ppermute | solution.py:289
  4.5 2.1 %collective-permute-done.u1 = bf16[272,256]{1,0:T(8,128)(2,1)S(1)} collective-permute-done((bf16[272,256]{1,0:T(8,128)(2,1)}, bf16[272,256]{1,0:T(8,128)(2,1)S(1)}, u32[]{:S(2)}, u32[]{:S(2)}) %collective-permute-start) | collective-permute-done | bytes 139296 | tf_op jit(solution)/shard_map/ppermute | solution.py:292
  6.5 1.5 %collective-permute-start.1 = (bf16[272,256]{1,0:T(8,128)(2,1)S(1)}, bf16[272,256]{1,0:T(8,128)(2,1)S(1)}, u32[]{:S(2)}, u32[]{:S(2)}) collective-permute-start(bf16[272,256]{1,0:T(8,128)(2,1)S(1)} %collective-permute-done.u1), channel_id=1, source_target_pairs={{0,32},{32,64},{64,96},{96,128},{128,160},{160,192},{192,224},{224... | collective-permute-start | bytes 417800 | tf_op jit(solution)/shard_map/ppermute | solution.py:292
  8.0 3.7 %collective-permute-start.8 = (bf16[272,256]{1,0:T(8,128)(2,1)}, bf16[272,256]{1,0:T(8,128)(2,1)S(1)}, u32[]{:S(2)}, u32[]{:S(2)}) collective-permute-start(bf16[272,256]{1,0:T(8,128)(2,1)} %pack.1.own_ref), channel_id=1, source_target_pairs={{0,128},{32,160},{64,192},{96,224},{128,0},{160,32},{192,64},{224,... | collective-permute-start | bytes 417800 | tf_op jit(solution)/shard_map/ppermute | solution.py:292
  11.7 0.0 collective-permute-done.4.d1
  11.7 0.0 collective-permute-start.5
  11.8 2.1 %collective-permute-start.14 = (bf16[272,256]{1,0:T(8,128)(2,1)S(1)}, bf16[272,256]{1,0:T(8,128)(2,1)S(1)}, u32[]{:S(2)}, u32[]{:S(2)}) collective-permute-start(bf16[272,256]{1,0:T(8,128)(2,1)S(1)} %collective-permute-done.u1), channel_id=1, source_target_pairs={{0,16},{16,0},{1,17},{17,1},{2,18},{18,2},{3,19},{19,3},{4,20},{20... | collective-permute-start | bytes 417800 | tf_op jit(solution)/shard_map/ppermute | solution.py:289
  13.8 0.0 copy-done
  13.8 0.0 copy-done.1
  13.8 0.0 copy-done.2
  13.9 0.0 copy-start.3
  13.9 0.9 %copy-done.3 = bf16[272,256]{1,0:T(8,128)(2,1)S(1)} copy-done((bf16[272,256]{1,0:T(8,128)(2,1)S(1)}, bf16[272,256]{1,0:T(8,128)(2,1)}, u32[]{:S(2)}) %copy-start.3) | copy-done | bytes 139288
  14.8 3.2 %shard_map.64 = (bf16[8,256,256]{2,1,0:T(8,128)(2,1)S(1)}, f32[8,256,128]{2,1,0:T(8,128)S(1)}, f32[8,256,256]{2,1,0:T(8,128)S(1)}, f32[8,256,256]{2,1,0:T(8,128)S(1)}) custom-call(bf16[272,256]{1,0:T(8,128)(2,1)S(1)} %copy-done.3, bf16[256,1024]{1,0:T(8,128)(2,1)S(1)} %copy-done, bf16[8,128,128]{2,1,0:T(8,128)(2,1)S(1)} %copy-done.2, ...), custom_call_target="tpu_custom_call" | custom-call | flops 786432000 | bytes 8388608 | tf_op jit(solution)/shard_map/pallas_call | solution.py:304
  17.9 0.0 collective-permute-done.13.pb
  17.9 0.1 collective-permute-start.12
  18.1 0.0 collective-permute-done.1.u2
  18.1 0.5 %collective-permute-start.10 = (bf16[272,256]{1,0:T(8,128)(2,1)S(1)}, bf16[272,256]{1,0:T(8,128)(2,1)S(1)}, u32[]{:S(2)}, u32[]{:S(2)}) collective-permute-start(bf16[272,256]{1,0:T(8,128)(2,1)S(1)} %collective-permute-done.1.u2), channel_id=1, source_target_pairs={{0,16},{16,0},{1,17},{17,1},{2,18},{18,2},{3,19},{19,3},{4,20},{20... | collective-permute-start | bytes 417800 | tf_op jit(solution)/shard_map/ppermute | solution.py:289
  18.5 0.0 collective-permute-done.8.x
  18.6 3.0 %collective-permute-start.2 = (bf16[272,256]{1,0:T(8,128)(2,1)S(1)}, bf16[272,256]{1,0:T(8,128)(2,1)S(1)}, u32[]{:S(2)}, u32[]{:S(2)}) collective-permute-start(bf16[272,256]{1,0:T(8,128)(2,1)S(1)} %collective-permute-done.1.u2), channel_id=1, source_target_pairs={{0,32},{32,64},{64,96},{96,128},{128,160},{160,192},{192,224},{224... | collective-permute-start | bytes 417800 | tf_op jit(solution)/shard_map/ppermute | solution.py:292
  21.5 0.2 collective-permute-done.5.d2
  21.7 1.1 %collective-permute-start.11 = (bf16[272,256]{1,0:T(8,128)(2,1)S(1)}, bf16[272,256]{1,0:T(8,128)(2,1)S(1)}, u32[]{:S(2)}, u32[]{:S(2)}) collective-permute-start(bf16[272,256]{1,0:T(8,128)(2,1)S(1)} %collective-permute-done.5.d2), channel_id=1, source_target_pairs={{0,16},{16,0},{1,17},{17,1},{2,18},{18,2},{3,19},{19,3},{4,20},{20... | collective-permute-start | bytes 417800 | tf_op jit(solution)/shard_map/ppermute | solution.py:289
  22.8 0.0 collective-permute-done.14.u1s
  22.8 0.9 %collective-permute-start.6 = (bf16[272,256]{1,0:T(8,128)(2,1)S(1)}, bf16[272,256]{1,0:T(8,128)(2,1)S(1)}, u32[]{:S(2)}, u32[]{:S(2)}) collective-permute-start(bf16[272,256]{1,0:T(8,128)(2,1)S(1)} %collective-permute-done.5.d2), channel_id=1, source_target_pairs={{0,224},{32,0},{64,32},{96,64},{128,96},{160,128},{192,160},{224,1... | collective-permute-start | bytes 417800 | tf_op jit(solution)/shard_map/ppermute | solution.py:292
  23.8 3.0 %shard_map.65 = (f32[8,256,128]{2,1,0:T(8,128)S(1)}, f32[8,256,256]{2,1,0:T(8,128)S(1)}, f32[256,256]{1,0:T(8,128)S(1)}) custom-call(bf16[272,256]{1,0:T(8,128)(2,1)S(1)} %collective-permute-done.13.pb, bf16[272,256]{1,0:T(8,128)(2,1)S(1)} %collective-permute-done.u1, ...), custom_call_target="tpu_custom_call", output_to_operand_aliasing={{0}: (5, {}), {1}: (6, {})} | custom-call | flops 1572864000 | bytes 8388608 | tf_op jit(solution)/shard_map/pallas_call | solution.py:315
  26.8 0.0 collective-permute-done.12.d1s
  26.8 0.4 collective-permute-start.9
  27.2 2.4 %shard_map.66 = (f32[8,256,128]{2,1,0:T(8,128)S(1)}, f32[8,256,256]{2,1,0:T(8,128)S(1)}, f32[256,256]{1,0:T(8,128)S(1)}) custom-call(bf16[272,256]{1,0:T(8,128)(2,1)S(1)} %collective-permute-done.4.d1, bf16[272,256]{1,0:T(8,128)(2,1)S(1)} %collective-permute-done.12.d1s, ...), custom_call_target="tpu_custom_call", output_to_operand_aliasing={{0}: (4, {}), {1}: (5, {}), {2}: (6, {})} | custom-call | flops 524288000 | bytes 8388608 | tf_op jit(solution)/shard_map/pallas_call | solution.py:322
  29.6 0.0 collective-permute-done.2.u3
  29.6 0.3 collective-permute-start.3
  29.9 0.0 collective-permute-done.6.d3
  29.9 0.3 collective-permute-start.7
  30.2 0.0 collective-permute-done.10.u2s
  30.2 0.0 collective-permute-done.11.d2s
  30.2 3.8 %shard_map.67 = (f32[8,256,128]{2,1,0:T(8,128)S(1)}, f32[8,256,256]{2,1,0:T(8,128)S(1)}, f32[256,256]{1,0:T(8,128)S(1)}) custom-call(bf16[272,256]{1,0:T(8,128)(2,1)S(1)} %collective-permute-done.1.u2, bf16[272,256]{1,0:T(8,128)(2,1)S(1)} %collective-permute-done.10.u2s, ...), custom_call_target="tpu_custom_call", output_to_operand_aliasing={{0}: (6, {}), {1}: (7, {}), {2}: (8, {})} | custom-call | flops 1572864000 | bytes 8388608 | tf_op jit(solution)/shard_map/pallas_call | solution.py:329
  34.0 0.0 collective-permute-done.9.xs
  34.0 2.4 %shard_map.68 = (f32[8,256,128]{2,1,0:T(8,128)S(1)}, f32[8,256,256]{2,1,0:T(8,128)S(1)}, f32[256,256]{1,0:T(8,128)S(1)}) custom-call(bf16[272,256]{1,0:T(8,128)(2,1)S(1)} %collective-permute-done.8.x, bf16[272,256]{1,0:T(8,128)(2,1)S(1)} %collective-permute-done.9.xs, ...), custom_call_target="tpu_custom_call", output_to_operand_aliasing={{0}: (4, {}), {1}: (5, {}), {2}: (6, {})} | custom-call | flops 786432000 | bytes 8388608 | tf_op jit(solution)/shard_map/pallas_call | solution.py:336
  36.4 0.0 collective-permute-done.3.u3s
  36.5 0.0 collective-permute-done.7.d3s
  36.5 4.7 %shard_map.69 = bf16[256,1024]{1,0:T(8,128)(2,1)} custom-call(bf16[272,256]{1,0:T(8,128)(2,1)S(1)} %collective-permute-done.2.u3, bf16[272,256]{1,0:T(8,128)(2,1)S(1)} %collective-permute-done.3.u3s, bf16[272,256]{1,0:T(8,128)(2,1)S(1)} %collective-permute-done.6.d3, bf16[272,256]{1,0:T(8,128)(2,1)S(1)} %collective-permute-done.7.d3s, ...), custom_call_target="tpu_custom_call" | custom-call | flops 1572864000 | bytes 8388608 | tf_op jit(solution)/shard_map/pallas_call | solution.py:343
Async XLA Ops:
  0.0 13.8 %copy-start = (bf16[256,1024]{1,0:T(8,128)(2,1)S(1)}, bf16[256,1024]{1,0:T(8,128)(2,1)}, u32[]{:S(2)}) copy-start(bf16[256,1024]{1,0:T(8,128)(2,1)} %q_ref.11) | copy-start | bytes 1572868
  0.0 13.8 %copy-start.1 = (bf16[8,128,128]{2,1,0:T(8,128)(2,1)S(1)}, bf16[8,128,128]{2,1,0:T(8,128)(2,1)}, u32[]{:S(2)}) copy-start(bf16[8,128,128]{2,1,0:T(8,128)(2,1)} %kmap_ref.11) | copy-start | bytes 786436
  0.0 13.8 %copy-start.2 = (bf16[8,128,128]{2,1,0:T(8,128)(2,1)S(1)}, bf16[8,128,128]{2,1,0:T(8,128)(2,1)}, u32[]{:S(2)}) copy-start(bf16[8,128,128]{2,1,0:T(8,128)(2,1)} %qmap_ref.1) | copy-start | bytes 786436
  1.7 4.8 %collective-permute-start = (bf16[272,256]{1,0:T(8,128)(2,1)}, bf16[272,256]{1,0:T(8,128)(2,1)S(1)}, u32[]{:S(2)}, u32[]{:S(2)}) collective-permute-start(bf16[272,256]{1,0:T(8,128)(2,1)} %pack.1.own_ref), channel_id=1, source_target_pairs={{0,32},{32,64},{64,96},{96,128},{128,160},{160,192},{192,224},{224... | collective-permute-start | bytes 417800 | tf_op jit(solution)/shard_map/ppermute | solution.py:292
  1.8 10.0 %collective-permute-start.4 = (bf16[272,256]{1,0:T(8,128)(2,1)}, bf16[272,256]{1,0:T(8,128)(2,1)S(1)}, u32[]{:S(2)}, u32[]{:S(2)}) collective-permute-start(bf16[272,256]{1,0:T(8,128)(2,1)} %pack.1.own_ref), channel_id=1, source_target_pairs={{0,224},{32,0},{64,32},{96,64},{128,96},{160,128},{192,160},{224,1... | collective-permute-start | bytes 417800 | tf_op jit(solution)/shard_map/ppermute | solution.py:292
  3.2 14.7 %collective-permute-start.13 = (bf16[272,256]{1,0:T(8,128)(2,1)}, bf16[272,256]{1,0:T(8,128)(2,1)S(1)}, u32[]{:S(2)}, u32[]{:S(2)}) collective-permute-start(bf16[272,256]{1,0:T(8,128)(2,1)} %pack.1.own_ref), channel_id=1, source_target_pairs={{0,16},{16,0},{1,17},{17,1},{2,18},{18,2},{3,19},{19,3},{4,20},{20... | collective-permute-start | bytes 417800 | tf_op jit(solution)/shard_map/ppermute | solution.py:289
  6.5 11.6 %collective-permute-start.1 = (bf16[272,256]{1,0:T(8,128)(2,1)S(1)}, bf16[272,256]{1,0:T(8,128)(2,1)S(1)}, u32[]{:S(2)}, u32[]{:S(2)}) collective-permute-start(bf16[272,256]{1,0:T(8,128)(2,1)S(1)} %collective-permute-done.u1), channel_id=1, source_target_pairs={{0,32},{32,64},{64,96},{96,128},{128,160},{160,192},{192,224},{224... | collective-permute-start | bytes 417800 | tf_op jit(solution)/shard_map/ppermute | solution.py:292
  8.0 10.5 %collective-permute-start.8 = (bf16[272,256]{1,0:T(8,128)(2,1)}, bf16[272,256]{1,0:T(8,128)(2,1)S(1)}, u32[]{:S(2)}, u32[]{:S(2)}) collective-permute-start(bf16[272,256]{1,0:T(8,128)(2,1)} %pack.1.own_ref), channel_id=1, source_target_pairs={{0,128},{32,160},{64,192},{96,224},{128,0},{160,32},{192,64},{224,... | collective-permute-start | bytes 417800 | tf_op jit(solution)/shard_map/ppermute | solution.py:292
  11.7 10.0 %collective-permute-start.5 = (bf16[272,256]{1,0:T(8,128)(2,1)S(1)}, bf16[272,256]{1,0:T(8,128)(2,1)S(1)}, u32[]{:S(2)}, u32[]{:S(2)}) collective-permute-start(bf16[272,256]{1,0:T(8,128)(2,1)S(1)} %collective-permute-done.4.d1), channel_id=1, source_target_pairs={{0,224},{32,0},{64,32},{96,64},{128,96},{160,128},{192,160},{224,1... | collective-permute-start | bytes 417800 | tf_op jit(solution)/shard_map/ppermute | solution.py:292
  11.8 11.1 %collective-permute-start.14 = (bf16[272,256]{1,0:T(8,128)(2,1)S(1)}, bf16[272,256]{1,0:T(8,128)(2,1)S(1)}, u32[]{:S(2)}, u32[]{:S(2)}) collective-permute-start(bf16[272,256]{1,0:T(8,128)(2,1)S(1)} %collective-permute-done.u1), channel_id=1, source_target_pairs={{0,16},{16,0},{1,17},{17,1},{2,18},{18,2},{3,19},{19,3},{4,20},{20... | collective-permute-start | bytes 417800 | tf_op jit(solution)/shard_map/ppermute | solution.py:289
  13.9 0.9 %copy-start.3 = (bf16[272,256]{1,0:T(8,128)(2,1)S(1)}, bf16[272,256]{1,0:T(8,128)(2,1)}, u32[]{:S(2)}) copy-start(bf16[272,256]{1,0:T(8,128)(2,1)} %pack.1.own_ref) | copy-start | bytes 417796
  17.9 8.8 %collective-permute-start.12 = (bf16[272,256]{1,0:T(8,128)(2,1)S(1)}, bf16[272,256]{1,0:T(8,128)(2,1)S(1)}, u32[]{:S(2)}, u32[]{:S(2)}) collective-permute-start(bf16[272,256]{1,0:T(8,128)(2,1)S(1)} %collective-permute-done.4.d1), channel_id=1, source_target_pairs={{0,16},{16,0},{1,17},{17,1},{2,18},{18,2},{3,19},{19,3},{4,20},{20... | collective-permute-start | bytes 417800 | tf_op jit(solution)/shard_map/ppermute | solution.py:289
  18.1 12.1 %collective-permute-start.10 = (bf16[272,256]{1,0:T(8,128)(2,1)S(1)}, bf16[272,256]{1,0:T(8,128)(2,1)S(1)}, u32[]{:S(2)}, u32[]{:S(2)}) collective-permute-start(bf16[272,256]{1,0:T(8,128)(2,1)S(1)} %collective-permute-done.1.u2), channel_id=1, source_target_pairs={{0,16},{16,0},{1,17},{17,1},{2,18},{18,2},{3,19},{19,3},{4,20},{20... | collective-permute-start | bytes 417800 | tf_op jit(solution)/shard_map/ppermute | solution.py:289
  18.6 11.0 %collective-permute-start.2 = (bf16[272,256]{1,0:T(8,128)(2,1)S(1)}, bf16[272,256]{1,0:T(8,128)(2,1)S(1)}, u32[]{:S(2)}, u32[]{:S(2)}) collective-permute-start(bf16[272,256]{1,0:T(8,128)(2,1)S(1)} %collective-permute-done.1.u2), channel_id=1, source_target_pairs={{0,32},{32,64},{64,96},{96,128},{128,160},{160,192},{192,224},{224... | collective-permute-start | bytes 417800 | tf_op jit(solution)/shard_map/ppermute | solution.py:292
  21.7 8.5 %collective-permute-start.11 = (bf16[272,256]{1,0:T(8,128)(2,1)S(1)}, bf16[272,256]{1,0:T(8,128)(2,1)S(1)}, u32[]{:S(2)}, u32[]{:S(2)}) collective-permute-start(bf16[272,256]{1,0:T(8,128)(2,1)S(1)} %collective-permute-done.5.d2), channel_id=1, source_target_pairs={{0,16},{16,0},{1,17},{17,1},{2,18},{18,2},{3,19},{19,3},{4,20},{20... | collective-permute-start | bytes 417800 | tf_op jit(solution)/shard_map/ppermute | solution.py:289
  22.8 7.1 %collective-permute-start.6 = (bf16[272,256]{1,0:T(8,128)(2,1)S(1)}, bf16[272,256]{1,0:T(8,128)(2,1)S(1)}, u32[]{:S(2)}, u32[]{:S(2)}) collective-permute-start(bf16[272,256]{1,0:T(8,128)(2,1)S(1)} %collective-permute-done.5.d2), channel_id=1, source_target_pairs={{0,224},{32,0},{64,32},{96,64},{128,96},{160,128},{192,160},{224,1... | collective-permute-start | bytes 417800 | tf_op jit(solution)/shard_map/ppermute | solution.py:292
  26.8 7.2 %collective-permute-start.9 = (bf16[272,256]{1,0:T(8,128)(2,1)S(1)}, bf16[272,256]{1,0:T(8,128)(2,1)S(1)}, u32[]{:S(2)}, u32[]{:S(2)}) collective-permute-start(bf16[272,256]{1,0:T(8,128)(2,1)S(1)} %collective-permute-done.8.x), channel_id=1, source_target_pairs={{0,16},{16,0},{1,17},{17,1},{2,18},{18,2},{3,19},{19,3},{4,20},{20... | collective-permute-start | bytes 417800 | tf_op jit(solution)/shard_map/ppermute | solution.py:289
  29.6 6.9 %collective-permute-start.3 = (bf16[272,256]{1,0:T(8,128)(2,1)S(1)}, bf16[272,256]{1,0:T(8,128)(2,1)S(1)}, u32[]{:S(2)}, u32[]{:S(2)}) collective-permute-start(bf16[272,256]{1,0:T(8,128)(2,1)S(1)} %collective-permute-done.2.u3), channel_id=1, source_target_pairs={{0,16},{16,0},{1,17},{17,1},{2,18},{18,2},{3,19},{19,3},{4,20},{20... | collective-permute-start | bytes 417800 | tf_op jit(solution)/shard_map/ppermute | solution.py:289
  29.9 6.6 %collective-permute-start.7 = (bf16[272,256]{1,0:T(8,128)(2,1)S(1)}, bf16[272,256]{1,0:T(8,128)(2,1)S(1)}, u32[]{:S(2)}, u32[]{:S(2)}) collective-permute-start(bf16[272,256]{1,0:T(8,128)(2,1)S(1)} %collective-permute-done.6.d3), channel_id=1, source_target_pairs={{0,16},{16,0},{1,17},{17,1},{2,18},{18,2},{3,19},{19,3},{4,20},{20... | collective-permute-start | bytes 417800 | tf_op jit(solution)/shard_map/ppermute | solution.py:289

commit v2 on v1

--- a/solution.py
+++ b/solution.py
@@ -173,30 +173,42 @@
     return state + nn(jnp.concatenate(feats, axis=1), va)
 
 
+def near_blocks(pb, u1, u1s):
+    z = lax.axis_index("z")
+    return [(pb, lax.axis_index("c") == 1), (u1, z >= 1), (u1s, z >= 1)]
+
+
+def early():
+    z = lax.axis_index("z")
+    return (z >= 3) & (z < 6)
+
+
 def near_kernel(pb, u1, u1s, q_ref, kmap_ref, m_in, accl_in, m_ref, accl_ref, state_ref):
-    z = lax.axis_index("z")
-    second = lax.axis_index("c") == 1
+    state_ref[...] = jnp.zeros_like(state_ref)
+
+    @pl.when(early())
+    def _():
+        state_ref[...] = absorb(
+            near_blocks(pb, u1, u1s), q_ref, kmap_ref, m_in, accl_in, 0.0, m_ref, accl_ref
+        )
+
+
+def wrap_kernel(pb, u1, u1s, d1, d1s, q_ref, kmap_ref, m_in, accl_in, state_in,
+                m_ref, accl_ref, state_ref):
+    z = lax.axis_index("z")
     ins = (q_ref, kmap_ref, m_in, accl_in)
-    outs = (m_ref, accl_ref)
-
-    @pl.when(z == 0)
-    def _():
-        state_ref[...] = absorb([(pb, second)], *ins, 0.0, *outs)
-
-    @pl.when(z >= 1)
-    def _():
-        blocks = [(pb, second), (u1, z >= 1), (u1s, z >= 1)]
-        state_ref[...] = absorb(blocks, *ins, 0.0, *outs)
-
-
-def wrap_kernel(d1, d1s, q_ref, kmap_ref, m_in, accl_in, state_in, m_ref, accl_ref, state_ref):
-    z = lax.axis_index("z")
+
+    @pl.when(jnp.logical_not(early()))
+    def _():
+        state_ref[...] = absorb(
+            near_blocks(pb, u1, u1s), *ins, state_in[...], m_ref, accl_ref
+        )
 
     @pl.when(z >= 7)
     def _():
         blocks = [(d1, z >= 7), (d1s, z >= 7)]
         state_ref[...] = absorb(
-            blocks, q_ref, kmap_ref, m_in, accl_in, state_in[...], m_ref, accl_ref
+            blocks, q_ref, kmap_ref, m_ref, accl_ref, state_ref[...], m_ref, accl_ref
         )
 
 
@@ -312,20 +324,21 @@
         flops=8 * 2 * 256 * 128 * 1500,
         nbytes=8 << 20,
     )(own, queries, query_map, key_map)
+    near = (swap(own), u1, swap(u1))
     m, accl, st = call(
         near_kernel,
         (heads(HD, f32), heads(256, f32), state),
         flops=8 * 2 * 256 * 128 * 3000,
         nbytes=8 << 20,
         aliases={5: 0, 6: 1},
-    )(swap(own), u1, swap(u1), queries, key_map, m, accl)
+    )(*near, queries, key_map, m, accl)
     m, accl, st = call(
         wrap_kernel,
         (heads(HD, f32), heads(256, f32), state),
         flops=8 * 2 * 256 * 128 * 1000,
         nbytes=8 << 20,
-        aliases={4: 0, 5: 1, 6: 2},
-    )(d1, swap(d1), queries, key_map, m, accl, st)
+        aliases={7: 0, 8: 1, 9: 2},
+    )(*near, d1, swap(d1), queries, key_map, m, accl, st)
     m, accl, st = call(
         mid_kernel,
         (heads(HD, f32), heads(256, f32), state),

time: 41.3 us -> 41.2 us (level)
  the two profiles are of different devices: /device:TPU:237 before, /device:TPU:231 now
where the time goes in v2:
time: 41.2 us; the launch traced here: 41.1 us
  Pallas kernels  20.9 us (51%)
  starting transfers between devices  16.8 us (41%)
  waiting for transfers between devices  2.32 us (6%)
  local copies, waits for them, and re-layouts  0.91 us (2%)
    ppermute x7, starting transfers between devices, hop(): return lax.ppermute(a, 'z', ring(shift))  10.6 us
    ppermute x8, starting transfers between devices, swap(): return lax.ppermute(a, 'c', SWAP)  6.18 us
    pallas_call x1, Pallas kernels, per_device(): call(wrap_kernel, (heads(HD, f32), heads(256, f32), state), flops=8 * 2 *...  4.96 us
    pallas_call x1, Pallas kernels, per_device(): call(last_kernel, jax.ShapeDtypeStruct((TOK, 8 * HD), bf16), flops=8 * 2...  4.72 us
    pallas_call x1, Pallas kernels, per_device(): call(mid_kernel, (heads(HD, f32), heads(256, f32), state), flops=8 * 2 *...  3.77 us
    pallas_call x1, Pallas kernels, per_device(): call(local_kernel, (heads(256, bf16), heads(HD, f32), heads(256, f32), he...  3.17 us
    pallas_call x1, Pallas kernels, per_device(): call(far_kernel, (heads(HD, f32), heads(256, f32), state), flops=8 * 2 *...  2.41 us
    ppermute x7, waiting for transfers between devices, hop(): return lax.ppermute(a, 'z', ring(shift))  2.29 us
  transfers between devices with their start and end apart: 15, of which 2 were waited for; matrix products, arithmetic and copies ran while one was open for 0% of the time, Pallas kernels for 35%

profile of v2, /device:TPU:231, one launch (start us, length us, event | category | flops | bytes accessed | tf_op | source)
XLA Modules:
  0.0 41.1 jit_solution(17103825164606368095)
XLA Ops:
  0.0 0.0 copy-start
  0.0 0.0 copy-start.1
  0.0 0.0 copy-start.2
  0.0 1.7 %pack.1.own_ref = bf16[272,256]{1,0:T(8,128)(2,1)} custom-call(bf16[256,1024]{1,0:T(8,128)(2,1)} %keys_ref.1, bf16[256,1024]{1,0:T(8,128)(2,1)} %values_ref.1, s32[1,256]{1,0:T(1,128)} %bitcast.1), custom_call_target="tpu_custom_call" | custom-call | flops 4294967296 | bytes 16777216 | tf_op jit(solution)/shard_map/pack/pallas_call | solution.py:290
  1.7 0.1 collective-permute-start
  1.8 1.5 %collective-permute-start.4 = (bf16[272,256]{1,0:T(8,128)(2,1)}, bf16[272,256]{1,0:T(8,128)(2,1)S(1)}, u32[]{:S(2)}, u32[]{:S(2)}) collective-permute-start(bf16[272,256]{1,0:T(8,128)(2,1)} %pack.1.own_ref), channel_id=1, source_target_pairs={{0,224},{32,0},{64,32},{96,64},{128,96},{160,128},{192,160},{224,1... | collective-permute-start | bytes 417800 | tf_op jit(solution)/shard_map/ppermute | solution.py:304
  3.2 1.2 %collective-permute-start.12 = (bf16[272,256]{1,0:T(8,128)(2,1)}, bf16[272,256]{1,0:T(8,128)(2,1)S(1)}, u32[]{:S(2)}, u32[]{:S(2)}) collective-permute-start(bf16[272,256]{1,0:T(8,128)(2,1)} %pack.1.own_ref), channel_id=1, source_target_pairs={{0,16},{16,0},{1,17},{17,1},{2,18},{18,2},{3,19},{19,3},{4,20},{20... | collective-permute-start | bytes 417800 | tf_op jit(solution)/shard_map/ppermute | solution.py:301
  4.5 2.1 %collective-permute-done.u1 = bf16[272,256]{1,0:T(8,128)(2,1)S(1)} collective-permute-done((bf16[272,256]{1,0:T(8,128)(2,1)}, bf16[272,256]{1,0:T(8,128)(2,1)S(1)}, u32[]{:S(2)}, u32[]{:S(2)}) %collective-permute-start) | collective-permute-done | bytes 139296 | tf_op jit(solution)/shard_map/ppermute | solution.py:304
  6.5 1.5 %collective-permute-start.1 = (bf16[272,256]{1,0:T(8,128)(2,1)S(1)}, bf16[272,256]{1,0:T(8,128)(2,1)S(1)}, u32[]{:S(2)}, u32[]{:S(2)}) collective-permute-start(bf16[272,256]{1,0:T(8,128)(2,1)S(1)} %collective-permute-done.u1), channel_id=1, source_target_pairs={{0,32},{32,64},{64,96},{96,128},{128,160},{160,192},{192,224},{224... | collective-permute-start | bytes 417800 | tf_op jit(solution)/shard_map/ppermute | solution.py:304
  8.0 3.7 %collective-permute-start.8 = (bf16[272,256]{1,0:T(8,128)(2,1)}, bf16[272,256]{1,0:T(8,128)(2,1)S(1)}, u32[]{:S(2)}, u32[]{:S(2)}) collective-permute-start(bf16[272,256]{1,0:T(8,128)(2,1)} %pack.1.own_ref), channel_id=1, source_target_pairs={{0,128},{32,160},{64,192},{96,224},{128,0},{160,32},{192,64},{224,... | collective-permute-start | bytes 417800 | tf_op jit(solution)/shard_map/ppermute | solution.py:304
  11.7 0.0 collective-permute-done.4.d1
  11.7 0.0 collective-permute-start.5
  11.8 2.1 %collective-permute-start.13 = (bf16[272,256]{1,0:T(8,128)(2,1)S(1)}, bf16[272,256]{1,0:T(8,128)(2,1)S(1)}, u32[]{:S(2)}, u32[]{:S(2)}) collective-permute-start(bf16[272,256]{1,0:T(8,128)(2,1)S(1)} %collective-permute-done.u1), channel_id=1, source_target_pairs={{0,16},{16,0},{1,17},{17,1},{2,18},{18,2},{3,19},{19,3},{4,20},{20... | collective-permute-start | bytes 417800 | tf_op jit(solution)/shard_map/ppermute | solution.py:301
  13.8 0.0 copy-done
  13.8 0.0 copy-done.1
  13.8 0.0 copy-done.2
  13.9 0.0 copy-start.3
  13.9 0.9 %copy-done.3 = bf16[272,256]{1,0:T(8,128)(2,1)S(1)} copy-done((bf16[272,256]{1,0:T(8,128)(2,1)S(1)}, bf16[272,256]{1,0:T(8,128)(2,1)}, u32[]{:S(2)}) %copy-start.3) | copy-done | bytes 139288
  14.8 3.2 %shard_map.64 = (bf16[8,256,256]{2,1,0:T(8,128)(2,1)S(1)}, f32[8,256,128]{2,1,0:T(8,128)S(1)}, f32[8,256,256]{2,1,0:T(8,128)S(1)}, f32[8,256,256]{2,1,0:T(8,128)S(1)}) custom-call(bf16[272,256]{1,0:T(8,128)(2,1)S(1)} %copy-done.3, bf16[256,1024]{1,0:T(8,128)(2,1)S(1)} %copy-done, bf16[8,128,128]{2,1,0:T(8,128)(2,1)S(1)} %copy-done.2, ...), custom_call_target="tpu_custom_call" | custom-call | flops 786432000 | bytes 8388608 | tf_op jit(solution)/shard_map/pallas_call | solution.py:316
  17.9 0.0 collective-permute-done.12.pb
  17.9 0.1 collective-permute-start.14
  18.1 0.0 collective-permute-done.1.u2
  18.1 0.5 %collective-permute-start.10 = (bf16[272,256]{1,0:T(8,128)(2,1)S(1)}, bf16[272,256]{1,0:T(8,128)(2,1)S(1)}, u32[]{:S(2)}, u32[]{:S(2)}) collective-permute-start(bf16[272,256]{1,0:T(8,128)(2,1)S(1)} %collective-permute-done.1.u2), channel_id=1, source_target_pairs={{0,16},{16,0},{1,17},{17,1},{2,18},{18,2},{3,19},{19,3},{4,20},{20... | collective-permute-start | bytes 417800 | tf_op jit(solution)/shard_map/ppermute | solution.py:301
  18.6 0.0 collective-permute-done.8.x
  18.6 3.0 %collective-permute-start.2 = (bf16[272,256]{1,0:T(8,128)(2,1)S(1)}, bf16[272,256]{1,0:T(8,128)(2,1)S(1)}, u32[]{:S(2)}, u32[]{:S(2)}) collective-permute-start(bf16[272,256]{1,0:T(8,128)(2,1)S(1)} %collective-permute-done.1.u2), channel_id=1, source_target_pairs={{0,32},{32,64},{64,96},{96,128},{128,160},{160,192},{192,224},{224... | collective-permute-start | bytes 417800 | tf_op jit(solution)/shard_map/ppermute | solution.py:304
  21.5 0.2 collective-permute-done.5.d2
  21.7 1.1 %collective-permute-start.11 = (bf16[272,256]{1,0:T(8,128)(2,1)S(1)}, bf16[272,256]{1,0:T(8,128)(2,1)S(1)}, u32[]{:S(2)}, u32[]{:S(2)}) collective-permute-start(bf16[272,256]{1,0:T(8,128)(2,1)S(1)} %collective-permute-done.5.d2), channel_id=1, source_target_pairs={{0,16},{16,0},{1,17},{17,1},{2,18},{18,2},{3,19},{19,3},{4,20},{20... | collective-permute-start | bytes 417800 | tf_op jit(solution)/shard_map/ppermute | solution.py:301
  22.8 0.0 collective-permute-done.13.u1s
  22.8 0.9 %collective-permute-start.6 = (bf16[272,256]{1,0:T(8,128)(2,1)S(1)}, bf16[272,256]{1,0:T(8,128)(2,1)S(1)}, u32[]{:S(2)}, u32[]{:S(2)}) collective-permute-start(bf16[272,256]{1,0:T(8,128)(2,1)S(1)} %collective-permute-done.5.d2), channel_id=1, source_target_pairs={{0,224},{32,0},{64,32},{96,64},{128,96},{160,128},{192,160},{224,1... | collective-permute-start | bytes 417800 | tf_op jit(solution)/shard_map/ppermute | solution.py:304
  23.8 0.2 shard_map.65
  24.0 0.0 collective-permute-done.14.d1s
  24.0 0.4 collective-permute-start.9
  24.3 5.0 %shard_map.66 = (f32[8,256,128]{2,1,0:T(8,128)S(1)}, f32[8,256,256]{2,1,0:T(8,128)S(1)}, f32[256,256]{1,0:T(8,128)S(1)}) custom-call(bf16[272,256]{1,0:T(8,128)(2,1)S(1)} %collective-permute-done.12.pb, bf16[272,256]{1,0:T(8,128)(2,1)S(1)} %collective-permute-done.u1, ...), custom_call_target="tpu_custom_call", output_to_operand_aliasing={{0}: (7, {}), {1}: (8, {}), {2}: (9, {})} | custom-call | flops 524288000 | bytes 8388608 | tf_op jit(solution)/shard_map/pallas_call | solution.py:335
  29.3 0.0 collective-permute-done.2.u3
  29.3 0.3 collective-permute-start.3
  29.6 0.0 collective-permute-done.6.d3
  29.6 0.5 %collective-permute-start.7 = (bf16[272,256]{1,0:T(8,128)(2,1)S(1)}, bf16[272,256]{1,0:T(8,128)(2,1)S(1)}, u32[]{:S(2)}, u32[]{:S(2)}) collective-permute-start(bf16[272,256]{1,0:T(8,128)(2,1)S(1)} %collective-permute-done.6.d3), channel_id=1, source_target_pairs={{0,16},{16,0},{1,17},{17,1},{2,18},{18,2},{3,19},{19,3},{4,20},{20... | collective-permute-start | bytes 417800 | tf_op jit(solution)/shard_map/ppermute | solution.py:301
  30.1 0.0 collective-permute-done.10.u2s
  30.1 0.0 collective-permute-done.11.d2s
  30.1 3.8 %shard_map.67 = (f32[8,256,128]{2,1,0:T(8,128)S(1)}, f32[8,256,256]{2,1,0:T(8,128)S(1)}, f32[256,256]{1,0:T(8,128)S(1)}) custom-call(bf16[272,256]{1,0:T(8,128)(2,1)S(1)} %collective-permute-done.1.u2, bf16[272,256]{1,0:T(8,128)(2,1)S(1)} %collective-permute-done.10.u2s, ...), custom_call_target="tpu_custom_call", output_to_operand_aliasing={{0}: (6, {}), {1}: (7, {}), {2}: (8, {})} | custom-call | flops 1572864000 | bytes 8388608 | tf_op jit(solution)/shard_map/pallas_call | solution.py:342
  33.9 0.0 collective-permute-done.9.xs
  33.9 2.4 %shard_map.68 = (f32[8,256,128]{2,1,0:T(8,128)S(1)}, f32[8,256,256]{2,1,0:T(8,128)S(1)}, f32[256,256]{1,0:T(8,128)S(1)}) custom-call(bf16[272,256]{1,0:T(8,128)(2,1)S(1)} %collective-permute-done.8.x, bf16[272,256]{1,0:T(8,128)(2,1)S(1)} %collective-permute-done.9.xs, ...), custom_call_target="tpu_custom_call", output_to_operand_aliasing={{0}: (4, {}), {1}: (5, {}), {2}: (6, {})} | custom-call | flops 786432000 | bytes 8388608 | tf_op jit(solution)/shard_map/pallas_call | solution.py:349
  36.3 0.0 collective-permute-done.3.u3s
  36.3 0.0 collective-permute-done.7.d3s
  36.4 4.7 %shard_map.69 = bf16[256,1024]{1,0:T(8,128)(2,1)} custom-call(bf16[272,256]{1,0:T(8,128)(2,1)S(1)} %collective-permute-done.2.u3, bf16[272,256]{1,0:T(8,128)(2,1)S(1)} %collective-permute-done.3.u3s, bf16[272,256]{1,0:T(8,128)(2,1)S(1)} %collective-permute-done.6.d3, bf16[272,256]{1,0:T(8,128)(2,1)S(1)} %collective-permute-done.7.d3s, ...), custom_call_target="tpu_custom_call" | custom-call | flops 1572864000 | bytes 8388608 | tf_op jit(solution)/shard_map/pallas_call | solution.py:356
Async XLA Ops:
  0.0 13.8 %copy-start = (bf16[256,1024]{1,0:T(8,128)(2,1)S(1)}, bf16[256,1024]{1,0:T(8,128)(2,1)}, u32[]{:S(2)}) copy-start(bf16[256,1024]{1,0:T(8,128)(2,1)} %q_ref.11) | copy-start | bytes 1572868
  0.0 13.8 %copy-start.1 = (bf16[8,128,128]{2,1,0:T(8,128)(2,1)S(1)}, bf16[8,128,128]{2,1,0:T(8,128)(2,1)}, u32[]{:S(2)}) copy-start(bf16[8,128,128]{2,1,0:T(8,128)(2,1)} %kmap_ref.11) | copy-start | bytes 786436
  0.0 13.8 %copy-start.2 = (bf16[8,128,128]{2,1,0:T(8,128)(2,1)S(1)}, bf16[8,128,128]{2,1,0:T(8,128)(2,1)}, u32[]{:S(2)}) copy-start(bf16[8,128,128]{2,1,0:T(8,128)(2,1)} %qmap_ref.1) | copy-start | bytes 786436
  1.7 4.8 %collective-permute-start = (bf16[272,256]{1,0:T(8,128)(2,1)}, bf16[272,256]{1,0:T(8,128)(2,1)S(1)}, u32[]{:S(2)}, u32[]{:S(2)}) collective-permute-start(bf16[272,256]{1,0:T(8,128)(2,1)} %pack.1.own_ref), channel_id=1, source_target_pairs={{0,32},{32,64},{64,96},{96,128},{128,160},{160,192},{192,224},{224... | collective-permute-start | bytes 417800 | tf_op jit(solution)/shard_map/ppermute | solution.py:304
  1.8 10.0 %collective-permute-start.4 = (bf16[272,256]{1,0:T(8,128)(2,1)}, bf16[272,256]{1,0:T(8,128)(2,1)S(1)}, u32[]{:S(2)}, u32[]{:S(2)}) collective-permute-start(bf16[272,256]{1,0:T(8,128)(2,1)} %pack.1.own_ref), channel_id=1, source_target_pairs={{0,224},{32,0},{64,32},{96,64},{128,96},{160,128},{192,160},{224,1... | collective-permute-start | bytes 417800 | tf_op jit(solution)/shard_map/ppermute | solution.py:304
  3.2 14.7 %collective-permute-start.12 = (bf16[272,256]{1,0:T(8,128)(2,1)}, bf16[272,256]{1,0:T(8,128)(2,1)S(1)}, u32[]{:S(2)}, u32[]{:S(2)}) collective-permute-start(bf16[272,256]{1,0:T(8,128)(2,1)} %pack.1.own_ref), channel_id=1, source_target_pairs={{0,16},{16,0},{1,17},{17,1},{2,18},{18,2},{3,19},{19,3},{4,20},{20... | collective-permute-start | bytes 417800 | tf_op jit(solution)/shard_map/ppermute | solution.py:301
  6.5 11.6 %collective-permute-start.1 = (bf16[272,256]{1,0:T(8,128)(2,1)S(1)}, bf16[272,256]{1,0:T(8,128)(2,1)S(1)}, u32[]{:S(2)}, u32[]{:S(2)}) collective-permute-start(bf16[272,256]{1,0:T(8,128)(2,1)S(1)} %collective-permute-done.u1), channel_id=1, source_target_pairs={{0,32},{32,64},{64,96},{96,128},{128,160},{160,192},{192,224},{224... | collective-permute-start | bytes 417800 | tf_op jit(solution)/shard_map/ppermute | solution.py:304
  8.0 10.5 %collective-permute-start.8 = (bf16[272,256]{1,0:T(8,128)(2,1)}, bf16[272,256]{1,0:T(8,128)(2,1)S(1)}, u32[]{:S(2)}, u32[]{:S(2)}) collective-permute-start(bf16[272,256]{1,0:T(8,128)(2,1)} %pack.1.own_ref), channel_id=1, source_target_pairs={{0,128},{32,160},{64,192},{96,224},{128,0},{160,32},{192,64},{224,... | collective-permute-start | bytes 417800 | tf_op jit(solution)/shard_map/ppermute | solution.py:304
  11.7 10.0 %collective-permute-start.5 = (bf16[272,256]{1,0:T(8,128)(2,1)S(1)}, bf16[272,256]{1,0:T(8,128)(2,1)S(1)}, u32[]{:S(2)}, u32[]{:S(2)}) collective-permute-start(bf16[272,256]{1,0:T(8,128)(2,1)S(1)} %collective-permute-done.4.d1), channel_id=1, source_target_pairs={{0,224},{32,0},{64,32},{96,64},{128,96},{160,128},{192,160},{224,1... | collective-permute-start | bytes 417800 | tf_op jit(solution)/shard_map/ppermute | solution.py:304
  11.8 11.1 %collective-permute-start.13 = (bf16[272,256]{1,0:T(8,128)(2,1)S(1)}, bf16[272,256]{1,0:T(8,128)(2,1)S(1)}, u32[]{:S(2)}, u32[]{:S(2)}) collective-permute-start(bf16[272,256]{1,0:T(8,128)(2,1)S(1)} %collective-permute-done.u1), channel_id=1, source_target_pairs={{0,16},{16,0},{1,17},{17,1},{2,18},{18,2},{3,19},{19,3},{4,20},{20... | collective-permute-start | bytes 417800 | tf_op jit(solution)/shard_map/ppermute | solution.py:301
  13.9 0.9 %copy-start.3 = (bf16[272,256]{1,0:T(8,128)(2,1)S(1)}, bf16[272,256]{1,0:T(8,128)(2,1)}, u32[]{:S(2)}) copy-start(bf16[272,256]{1,0:T(8,128)(2,1)} %pack.1.own_ref) | copy-start | bytes 417796
  17.9 6.0 %collective-permute-start.14 = (bf16[272,256]{1,0:T(8,128)(2,1)S(1)}, bf16[272,256]{1,0:T(8,128)(2,1)S(1)}, u32[]{:S(2)}, u32[]{:S(2)}) collective-permute-start(bf16[272,256]{1,0:T(8,128)(2,1)S(1)} %collective-permute-done.4.d1), channel_id=1, source_target_pairs={{0,16},{16,0},{1,17},{17,1},{2,18},{18,2},{3,19},{19,3},{4,20},{20... | collective-permute-start | bytes 417800 | tf_op jit(solution)/shard_map/ppermute | solution.py:301
  18.1 12.0 %collective-permute-start.10 = (bf16[272,256]{1,0:T(8,128)(2,1)S(1)}, bf16[272,256]{1,0:T(8,128)(2,1)S(1)}, u32[]{:S(2)}, u32[]{:S(2)}) collective-permute-start(bf16[272,256]{1,0:T(8,128)(2,1)S(1)} %collective-permute-done.1.u2), channel_id=1, source_target_pairs={{0,16},{16,0},{1,17},{17,1},{2,18},{18,2},{3,19},{19,3},{4,20},{20... | collective-permute-start | bytes 417800 | tf_op jit(solution)/shard_map/ppermute | solution.py:301
  18.6 10.8 %collective-permute-start.2 = (bf16[272,256]{1,0:T(8,128)(2,1)S(1)}, bf16[272,256]{1,0:T(8,128)(2,1)S(1)}, u32[]{:S(2)}, u32[]{:S(2)}) collective-permute-start(bf16[272,256]{1,0:T(8,128)(2,1)S(1)} %collective-permute-done.1.u2), channel_id=1, source_target_pairs={{0,32},{32,64},{64,96},{96,128},{128,160},{160,192},{192,224},{224... | collective-permute-start | bytes 417800 | tf_op jit(solution)/shard_map/ppermute | solution.py:304
  21.7 8.4 %collective-permute-start.11 = (bf16[272,256]{1,0:T(8,128)(2,1)S(1)}, bf16[272,256]{1,0:T(8,128)(2,1)S(1)}, u32[]{:S(2)}, u32[]{:S(2)}) collective-permute-start(bf16[272,256]{1,0:T(8,128)(2,1)S(1)} %collective-permute-done.5.d2), channel_id=1, source_target_pairs={{0,16},{16,0},{1,17},{17,1},{2,18},{18,2},{3,19},{19,3},{4,20},{20... | collective-permute-start | bytes 417800 | tf_op jit(solution)/shard_map/ppermute | solution.py:301
  22.8 6.8 %collective-permute-start.6 = (bf16[272,256]{1,0:T(8,128)(2,1)S(1)}, bf16[272,256]{1,0:T(8,128)(2,1)S(1)}, u32[]{:S(2)}, u32[]{:S(2)}) collective-permute-start(bf16[272,256]{1,0:T(8,128)(2,1)S(1)} %collective-permute-done.5.d2), channel_id=1, source_target_pairs={{0,224},{32,0},{64,32},{96,64},{128,96},{160,128},{192,160},{224,1... | collective-permute-start | bytes 417800 | tf_op jit(solution)/shard_map/ppermute | solution.py:304
  24.0 9.9 %collective-permute-start.9 = (bf16[272,256]{1,0:T(8,128)(2,1)S(1)}, bf16[272,256]{1,0:T(8,128)(2,1)S(1)}, u32[]{:S(2)}, u32[]{:S(2)}) collective-permute-start(bf16[272,256]{1,0:T(8,128)(2,1)S(1)} %collective-permute-done.8.x), channel_id=1, source_target_pairs={{0,16},{16,0},{1,17},{17,1},{2,18},{18,2},{3,19},{19,3},{4,20},{20... | collective-permute-start | bytes 417800 | tf_op jit(solution)/shard_map/ppermute | solution.py:301
  29.3 7.0 %collective-permute-start.3 = (bf16[272,256]{1,0:T(8,128)(2,1)S(1)}, bf16[272,256]{1,0:T(8,128)(2,1)S(1)}, u32[]{:S(2)}, u32[]{:S(2)}) collective-permute-start(bf16[272,256]{1,0:T(8,128)(2,1)S(1)} %collective-permute-done.2.u3), channel_id=1, source_target_pairs={{0,16},{16,0},{1,17},{17,1},{2,18},{18,2},{3,19},{19,3},{4,20},{20... | collective-permute-start | bytes 417800 | tf_op jit(solution)/shard_map/ppermute | solution.py:301
  29.6 6.7 %collective-permute-start.7 = (bf16[272,256]{1,0:T(8,128)(2,1)S(1)}, bf16[272,256]{1,0:T(8,128)(2,1)S(1)}, u32[]{:S(2)}, u32[]{:S(2)}) collective-permute-start(bf16[272,256]{1,0:T(8,128)(2,1)S(1)} %collective-permute-done.6.d3), channel_id=1, source_target_pairs={{0,16},{16,0},{1,17},{17,1},{2,18},{18,2},{3,19},{19,3},{4,20},{20... | collective-permute-start | bytes 417800 | tf_op jit(solution)/shard_map/ppermute | solution.py:301

commit v3 on v1

--- a/solution.py
+++ b/solution.py
@@ -173,7 +173,7 @@
     return state + nn(jnp.concatenate(feats, axis=1), va)
 
 
-def near_kernel(pb, u1, u1s, q_ref, kmap_ref, m_in, accl_in, m_ref, accl_ref, state_ref):
+def near_kernel(pb, u1, u1s, d1, d1s, q_ref, kmap_ref, m_in, accl_in, m_ref, accl_ref, state_ref):
     z = lax.axis_index("z")
     second = lax.axis_index("c") == 1
     ins = (q_ref, kmap_ref, m_in, accl_in)
@@ -188,16 +188,10 @@
         blocks = [(pb, second), (u1, z >= 1), (u1s, z >= 1)]
         state_ref[...] = absorb(blocks, *ins, 0.0, *outs)
 
-
-def wrap_kernel(d1, d1s, q_ref, kmap_ref, m_in, accl_in, state_in, m_ref, accl_ref, state_ref):
-    z = lax.axis_index("z")
-
     @pl.when(z >= 7)
     def _():
         blocks = [(d1, z >= 7), (d1s, z >= 7)]
-        state_ref[...] = absorb(
-            blocks, q_ref, kmap_ref, m_in, accl_in, state_in[...], m_ref, accl_ref
-        )
+        state_ref[...] = absorb(blocks, q_ref, kmap_ref, m_ref, accl_ref, state_ref[...], *outs)
 
 
 def mid_kernel(u2, u2s, d2, d2s, q_ref, kmap_ref, m_in, accl_in, state_in,
@@ -317,15 +311,8 @@
         (heads(HD, f32), heads(256, f32), state),
         flops=8 * 2 * 256 * 128 * 3000,
         nbytes=8 << 20,
-        aliases={5: 0, 6: 1},
-    )(swap(own), u1, swap(u1), queries, key_map, m, accl)
-    m, accl, st = call(
-        wrap_kernel,
-        (heads(HD, f32), heads(256, f32), state),
-        flops=8 * 2 * 256 * 128 * 1000,
-        nbytes=8 << 20,
-        aliases={4: 0, 5: 1, 6: 2},
-    )(d1, swap(d1), queries, key_map, m, accl, st)
+        aliases={7: 0, 8: 1},
+    )(swap(own), u1, swap(u1), d1, swap(d1), queries, key_map, m, accl)
     m, accl, st = call(
         mid_kernel,
         (heads(HD, f32), heads(256, f32), state),

time: 41.3 us -> 38.6 us (0.935)
  the two profiles are of different devices: /device:TPU:237 before, /device:TPU:99 now
where the time goes in v3:
time: 38.6 us; the launch traced here: 38.5 us
  starting transfers between devices  20.8 us (54%)
  Pallas kernels  13.8 us (36%)
  waiting for transfers between devices  2.86 us (7%)
  local copies, waits for them, and re-layouts  0.91 us (2%)
    ppermute x7, starting transfers between devices, hop(): return lax.ppermute(a, 'z', ring(shift))  10.9 us
    ppermute x8, starting transfers between devices, swap(): return lax.ppermute(a, 'c', SWAP)  9.89 us
    pallas_call x1, Pallas kernels, per_device(): call(last_kernel, jax.ShapeDtypeStruct((TOK, 8 * HD), bf16), flops=8 * 2...  3.26 us
    pallas_call x1, Pallas kernels, per_device(): call(local_kernel, (heads(256, bf16), heads(HD, f32), heads(256, f32), he...  3.22 us
    pallas_call x1, Pallas kernels, per_device(): call(near_kernel, (heads(HD, f32), heads(256, f32), state), flops=8 * 2 *...  2.94 us
    ppermute x7, waiting for transfers between devices, hop(): return lax.ppermute(a, 'z', ring(shift))  2.84 us
    pallas_call x1, Pallas kernels, per_device(): call(mid_kernel, (heads(HD, f32), heads(256, f32), state), flops=8 * 2 *...  2.7 us
    pallas_call x1, Pallas kernels, per_device(): pl.pallas_call(pack_kernel, out_shape=jax.ShapeDtypeStruct((ROWS, 2 * HD)...  1.66 us
  transfers between devices with their start and end apart: 15, of which 1 were waited for; matrix products, arithmetic and copies ran while one was open for 0% of the time, Pallas kernels for 23%

profile of v3, /device:TPU:99, one launch (start us, length us, event | category | flops | bytes accessed | tf_op | source)
XLA Modules:
  0.0 38.5 jit_solution(18433862285432307578)
XLA Ops:
  0.0 0.0 copy-start
  0.0 0.0 copy-start.1
  0.0 0.0 copy-start.2
  0.0 1.7 %pack.1.own_ref = bf16[272,256]{1,0:T(8,128)(2,1)} custom-call(bf16[256,1024]{1,0:T(8,128)(2,1)} %keys_ref.1, bf16[256,1024]{1,0:T(8,128)(2,1)} %values_ref.1, s32[1,256]{1,0:T(1,128)} %bitcast.1), custom_call_target="tpu_custom_call" | custom-call | flops 4294967296 | bytes 16777216 | tf_op jit(solution)/shard_map/pack/pallas_call | solution.py:272
  1.7 2.9 %collective-permute-start = (bf16[272,256]{1,0:T(8,128)(2,1)}, bf16[272,256]{1,0:T(8,128)(2,1)S(1)}, u32[]{:S(2)}, u32[]{:S(2)}) collective-permute-start(bf16[272,256]{1,0:T(8,128)(2,1)} %pack.1.own_ref), channel_id=1, source_target_pairs={{0,32},{32,64},{64,96},{96,128},{128,160},{160,192},{192,224},{224... | collective-permute-start | bytes 417800 | tf_op jit(solution)/shard_map/ppermute | solution.py:286
  4.6 0.0 collective-permute-start.4
  4.6 1.0 %collective-permute-start.12 = (bf16[272,256]{1,0:T(8,128)(2,1)}, bf16[272,256]{1,0:T(8,128)(2,1)S(1)}, u32[]{:S(2)}, u32[]{:S(2)}) collective-permute-start(bf16[272,256]{1,0:T(8,128)(2,1)} %pack.1.own_ref), channel_id=1, source_target_pairs={{0,16},{16,0},{1,17},{17,1},{2,18},{18,2},{3,19},{19,3},{4,20},{20... | collective-permute-start | bytes 417800 | tf_op jit(solution)/shard_map/ppermute | solution.py:283
  5.6 3.1 %collective-permute-start.8 = (bf16[272,256]{1,0:T(8,128)(2,1)}, bf16[272,256]{1,0:T(8,128)(2,1)S(1)}, u32[]{:S(2)}, u32[]{:S(2)}) collective-permute-start(bf16[272,256]{1,0:T(8,128)(2,1)} %pack.1.own_ref), channel_id=1, source_target_pairs={{0,128},{32,160},{64,192},{96,224},{128,0},{160,32},{192,64},{224,... | collective-permute-start | bytes 417800 | tf_op jit(solution)/shard_map/ppermute | solution.py:286
  8.7 0.0 collective-permute-done.u1
  8.7 1.9 %collective-permute-start.1 = (bf16[272,256]{1,0:T(8,128)(2,1)S(1)}, bf16[272,256]{1,0:T(8,128)(2,1)S(1)}, u32[]{:S(2)}, u32[]{:S(2)}) collective-permute-start(bf16[272,256]{1,0:T(8,128)(2,1)S(1)} %collective-permute-done.u1), channel_id=1, source_target_pairs={{0,32},{32,64},{64,96},{96,128},{128,160},{160,192},{192,224},{224... | collective-permute-start | bytes 417800 | tf_op jit(solution)/shard_map/ppermute | solution.py:286
  10.6 1.8 %collective-permute-start.13 = (bf16[272,256]{1,0:T(8,128)(2,1)S(1)}, bf16[272,256]{1,0:T(8,128)(2,1)S(1)}, u32[]{:S(2)}, u32[]{:S(2)}) collective-permute-start(bf16[272,256]{1,0:T(8,128)(2,1)S(1)} %collective-permute-done.u1), channel_id=1, source_target_pairs={{0,16},{16,0},{1,17},{17,1},{2,18},{18,2},{3,19},{19,3},{4,20},{20... | collective-permute-start | bytes 417800 | tf_op jit(solution)/shard_map/ppermute | solution.py:283
  12.4 0.0 collective-permute-done.4.d1
  12.4 0.0 collective-permute-start.5
  12.4 0.0 collective-permute-done.12.pb
  12.4 4.6 %collective-permute-start.14 = (bf16[272,256]{1,0:T(8,128)(2,1)S(1)}, bf16[272,256]{1,0:T(8,128)(2,1)S(1)}, u32[]{:S(2)}, u32[]{:S(2)}) collective-permute-start(bf16[272,256]{1,0:T(8,128)(2,1)S(1)} %collective-permute-done.4.d1), channel_id=1, source_target_pairs={{0,16},{16,0},{1,17},{17,1},{2,18},{18,2},{3,19},{19,3},{4,20},{20... | collective-permute-start | bytes 417800 | tf_op jit(solution)/shard_map/ppermute | solution.py:283
  17.0 0.0 copy-done
  17.0 0.0 copy-done.1
  17.0 0.0 copy-done.2
  17.0 0.0 copy-start.3
  17.0 0.9 %copy-done.3 = bf16[272,256]{1,0:T(8,128)(2,1)S(1)} copy-done((bf16[272,256]{1,0:T(8,128)(2,1)S(1)}, bf16[272,256]{1,0:T(8,128)(2,1)}, u32[]{:S(2)}) %copy-start.3) | copy-done | bytes 139288
  17.9 3.2 %shard_map.64 = (bf16[8,256,256]{2,1,0:T(8,128)(2,1)S(1)}, f32[8,256,128]{2,1,0:T(8,128)S(1)}, f32[8,256,256]{2,1,0:T(8,128)S(1)}, f32[8,256,256]{2,1,0:T(8,128)S(1)}) custom-call(bf16[272,256]{1,0:T(8,128)(2,1)S(1)} %copy-done.3, bf16[256,1024]{1,0:T(8,128)(2,1)S(1)} %copy-done, bf16[8,128,128]{2,1,0:T(8,128)(2,1)S(1)} %copy-done.2, ...), custom_call_target="tpu_custom_call" | custom-call | flops 786432000 | bytes 8388608 | tf_op jit(solution)/shard_map/pallas_call | solution.py:298
  21.2 0.0 collective-permute-done.8.x
  21.2 0.1 collective-permute-start.9
  21.3 0.0 collective-permute-done.1.u2
  21.3 0.5 %collective-permute-start.10 = (bf16[272,256]{1,0:T(8,128)(2,1)S(1)}, bf16[272,256]{1,0:T(8,128)(2,1)S(1)}, u32[]{:S(2)}, u32[]{:S(2)}) collective-permute-start(bf16[272,256]{1,0:T(8,128)(2,1)S(1)} %collective-permute-done.1.u2), channel_id=1, source_target_pairs={{0,16},{16,0},{1,17},{17,1},{2,18},{18,2},{3,19},{19,3},{4,20},{20... | collective-permute-start | bytes 417800 | tf_op jit(solution)/shard_map/ppermute | solution.py:283
  21.8 0.0 collective-permute-done.13.u1s
  21.8 3.0 %collective-permute-start.2 = (bf16[272,256]{1,0:T(8,128)(2,1)S(1)}, bf16[272,256]{1,0:T(8,128)(2,1)S(1)}, u32[]{:S(2)}, u32[]{:S(2)}) collective-permute-start(bf16[272,256]{1,0:T(8,128)(2,1)S(1)} %collective-permute-done.1.u2), channel_id=1, source_target_pairs={{0,32},{32,64},{64,96},{96,128},{128,160},{160,192},{192,224},{224... | collective-permute-start | bytes 417800 | tf_op jit(solution)/shard_map/ppermute | solution.py:286
  24.7 0.0 collective-permute-done.5.d2
  24.7 0.4 %collective-permute-start.11 = (bf16[272,256]{1,0:T(8,128)(2,1)S(1)}, bf16[272,256]{1,0:T(8,128)(2,1)S(1)}, u32[]{:S(2)}, u32[]{:S(2)}) collective-permute-start(bf16[272,256]{1,0:T(8,128)(2,1)S(1)} %collective-permute-done.5.d2), channel_id=1, source_target_pairs={{0,16},{16,0},{1,17},{17,1},{2,18},{18,2},{3,19},{19,3},{4,20},{20... | collective-permute-start | bytes 417800 | tf_op jit(solution)/shard_map/ppermute | solution.py:283
  25.1 0.0 collective-permute-done.14.d1s
  25.1 0.0 collective-permute-start.6
  25.1 2.9 %shard_map.65 = (f32[8,256,128]{2,1,0:T(8,128)S(1)}, f32[8,256,256]{2,1,0:T(8,128)S(1)}, f32[256,256]{1,0:T(8,128)S(1)}) custom-call(bf16[272,256]{1,0:T(8,128)(2,1)S(1)} %collective-permute-done.12.pb, bf16[272,256]{1,0:T(8,128)(2,1)S(1)} %collective-permute-done.u1, ...), custom_call_target="tpu_custom_call", output_to_operand_aliasing={{0}: (7, {}), {1}: (8, {})} | custom-call | flops 1572864000 | bytes 8388608 | tf_op jit(solution)/shard_map/pallas_call | solution.py:309
  28.1 0.0 collective-permute-done.2.u3
  28.1 0.5 %collective-permute-start.3 = (bf16[272,256]{1,0:T(8,128)(2,1)S(1)}, bf16[272,256]{1,0:T(8,128)(2,1)S(1)}, u32[]{:S(2)}, u32[]{:S(2)}) collective-permute-start(bf16[272,256]{1,0:T(8,128)(2,1)S(1)} %collective-permute-done.2.u3), channel_id=1, source_target_pairs={{0,16},{16,0},{1,17},{17,1},{2,18},{18,2},{3,19},{19,3},{4,20},{20... | collective-permute-start | bytes 417800 | tf_op jit(solution)/shard_map/ppermute | solution.py:283
  28.6 2.8 %collective-permute-done.6.d3 = bf16[272,256]{1,0:T(8,128)(2,1)S(1)} collective-permute-done((bf16[272,256]{1,0:T(8,128)(2,1)S(1)}, bf16[272,256]{1,0:T(8,128)(2,1)S(1)}, u32[]{:S(2)}, u32[]{:S(2)}) %collective-permute-start.6) | collective-permute-done | bytes 139296 | tf_op jit(solution)/shard_map/ppermute | solution.py:286
  31.5 1.0 %collective-permute-start.7 = (bf16[272,256]{1,0:T(8,128)(2,1)S(1)}, bf16[272,256]{1,0:T(8,128)(2,1)S(1)}, u32[]{:S(2)}, u32[]{:S(2)}) collective-permute-start(bf16[272,256]{1,0:T(8,128)(2,1)S(1)} %collective-permute-done.6.d3), channel_id=1, source_target_pairs={{0,16},{16,0},{1,17},{17,1},{2,18},{18,2},{3,19},{19,3},{4,20},{20... | collective-permute-start | bytes 417800 | tf_op jit(solution)/shard_map/ppermute | solution.py:283
  32.4 0.0 collective-permute-done.10.u2s
  32.4 0.0 collective-permute-done.11.d2s
  32.4 2.7 %shard_map.66 = (f32[8,256,128]{2,1,0:T(8,128)S(1)}, f32[8,256,256]{2,1,0:T(8,128)S(1)}, f32[256,256]{1,0:T(8,128)S(1)}) custom-call(bf16[272,256]{1,0:T(8,128)(2,1)S(1)} %collective-permute-done.1.u2, bf16[272,256]{1,0:T(8,128)(2,1)S(1)} %collective-permute-done.10.u2s, ...), custom_call_target="tpu_custom_call", output_to_operand_aliasing={{0}: (6, {}), {1}: (7, {}), {2}: (8, {})} | custom-call | flops 1572864000 | bytes 8388608 | tf_op jit(solution)/shard_map/pallas_call | solution.py:316
  35.1 0.0 collective-permute-done.9.xs
  35.2 0.0 collective-permute-done.3.u3s
  35.2 0.0 collective-permute-done.7.d3s
  35.2 3.3 %shard_map.68 = bf16[256,1024]{1,0:T(8,128)(2,1)} custom-call(bf16[272,256]{1,0:T(8,128)(2,1)S(1)} %collective-permute-done.2.u3, bf16[272,256]{1,0:T(8,128)(2,1)S(1)} %collective-permute-done.3.u3s, bf16[272,256]{1,0:T(8,128)(2,1)S(1)} %collective-permute-done.6.d3, bf16[272,256]{1,0:T(8,128)(2,1)S(1)} %collective-permute-done.7.d3s, ...), custom_call_target="tpu_custom_call" | custom-call | flops 1572864000 | bytes 8388608 | tf_op jit(solution)/shard_map/pallas_call | solution.py:330
  (1 shorter events, 0.0 us)
Async XLA Ops:
  0.0 17.0 %copy-start = (bf16[256,1024]{1,0:T(8,128)(2,1)S(1)}, bf16[256,1024]{1,0:T(8,128)(2,1)}, u32[]{:S(2)}) copy-start(bf16[256,1024]{1,0:T(8,128)(2,1)} %q_ref.9) | copy-start | bytes 1572868
  0.0 17.0 %copy-start.1 = (bf16[8,128,128]{2,1,0:T(8,128)(2,1)S(1)}, bf16[8,128,128]{2,1,0:T(8,128)(2,1)}, u32[]{:S(2)}) copy-start(bf16[8,128,128]{2,1,0:T(8,128)(2,1)} %kmap_ref.9) | copy-start | bytes 786436
  0.0 17.0 %copy-start.2 = (bf16[8,128,128]{2,1,0:T(8,128)(2,1)S(1)}, bf16[8,128,128]{2,1,0:T(8,128)(2,1)}, u32[]{:S(2)}) copy-start(bf16[8,128,128]{2,1,0:T(8,128)(2,1)} %qmap_ref.1) | copy-start | bytes 786436
  1.7 7.0 %collective-permute-start = (bf16[272,256]{1,0:T(8,128)(2,1)}, bf16[272,256]{1,0:T(8,128)(2,1)S(1)}, u32[]{:S(2)}, u32[]{:S(2)}) collective-permute-start(bf16[272,256]{1,0:T(8,128)(2,1)} %pack.1.own_ref), channel_id=1, source_target_pairs={{0,32},{32,64},{64,96},{96,128},{128,160},{160,192},{192,224},{224... | collective-permute-start | bytes 417800 | tf_op jit(solution)/shard_map/ppermute | solution.py:286
  4.6 7.8 %collective-permute-start.4 = (bf16[272,256]{1,0:T(8,128)(2,1)}, bf16[272,256]{1,0:T(8,128)(2,1)S(1)}, u32[]{:S(2)}, u32[]{:S(2)}) collective-permute-start(bf16[272,256]{1,0:T(8,128)(2,1)} %pack.1.own_ref), channel_id=1, source_target_pairs={{0,224},{32,0},{64,32},{96,64},{128,96},{160,128},{192,160},{224,1... | collective-permute-start | bytes 417800 | tf_op jit(solution)/shard_map/ppermute | solution.py:286
  4.6 7.8 %collective-permute-start.12 = (bf16[272,256]{1,0:T(8,128)(2,1)}, bf16[272,256]{1,0:T(8,128)(2,1)S(1)}, u32[]{:S(2)}, u32[]{:S(2)}) collective-permute-start(bf16[272,256]{1,0:T(8,128)(2,1)} %pack.1.own_ref), channel_id=1, source_target_pairs={{0,16},{16,0},{1,17},{17,1},{2,18},{18,2},{3,19},{19,3},{4,20},{20... | collective-permute-start | bytes 417800 | tf_op jit(solution)/shard_map/ppermute | solution.py:283
  5.6 15.6 %collective-permute-start.8 = (bf16[272,256]{1,0:T(8,128)(2,1)}, bf16[272,256]{1,0:T(8,128)(2,1)S(1)}, u32[]{:S(2)}, u32[]{:S(2)}) collective-permute-start(bf16[272,256]{1,0:T(8,128)(2,1)} %pack.1.own_ref), channel_id=1, source_target_pairs={{0,128},{32,160},{64,192},{96,224},{128,0},{160,32},{192,64},{224,... | collective-permute-start | bytes 417800 | tf_op jit(solution)/shard_map/ppermute | solution.py:286
  8.7 12.6 %collective-permute-start.1 = (bf16[272,256]{1,0:T(8,128)(2,1)S(1)}, bf16[272,256]{1,0:T(8,128)(2,1)S(1)}, u32[]{:S(2)}, u32[]{:S(2)}) collective-permute-start(bf16[272,256]{1,0:T(8,128)(2,1)S(1)} %collective-permute-done.u1), channel_id=1, source_target_pairs={{0,32},{32,64},{64,96},{96,128},{128,160},{160,192},{192,224},{224... | collective-permute-start | bytes 417800 | tf_op jit(solution)/shard_map/ppermute | solution.py:286
  10.6 11.2 %collective-permute-start.13 = (bf16[272,256]{1,0:T(8,128)(2,1)S(1)}, bf16[272,256]{1,0:T(8,128)(2,1)S(1)}, u32[]{:S(2)}, u32[]{:S(2)}) collective-permute-start(bf16[272,256]{1,0:T(8,128)(2,1)S(1)} %collective-permute-done.u1), channel_id=1, source_target_pairs={{0,16},{16,0},{1,17},{17,1},{2,18},{18,2},{3,19},{19,3},{4,20},{20... | collective-permute-start | bytes 417800 | tf_op jit(solution)/shard_map/ppermute | solution.py:283
  12.4 12.3 %collective-permute-start.5 = (bf16[272,256]{1,0:T(8,128)(2,1)S(1)}, bf16[272,256]{1,0:T(8,128)(2,1)S(1)}, u32[]{:S(2)}, u32[]{:S(2)}) collective-permute-start(bf16[272,256]{1,0:T(8,128)(2,1)S(1)} %collective-permute-done.4.d1), channel_id=1, source_target_pairs={{0,224},{32,0},{64,32},{96,64},{128,96},{160,128},{192,160},{224,1... | collective-permute-start | bytes 417800 | tf_op jit(solution)/shard_map/ppermute | solution.py:286
  12.4 12.7 %collective-permute-start.14 = (bf16[272,256]{1,0:T(8,128)(2,1)S(1)}, bf16[272,256]{1,0:T(8,128)(2,1)S(1)}, u32[]{:S(2)}, u32[]{:S(2)}) collective-permute-start(bf16[272,256]{1,0:T(8,128)(2,1)S(1)} %collective-permute-done.4.d1), channel_id=1, source_target_pairs={{0,16},{16,0},{1,17},{17,1},{2,18},{18,2},{3,19},{19,3},{4,20},{20... | collective-permute-start | bytes 417800 | tf_op jit(solution)/shard_map/ppermute | solution.py:283
  17.0 0.9 %copy-start.3 = (bf16[272,256]{1,0:T(8,128)(2,1)S(1)}, bf16[272,256]{1,0:T(8,128)(2,1)}, u32[]{:S(2)}) copy-start(bf16[272,256]{1,0:T(8,128)(2,1)} %pack.1.own_ref) | copy-start | bytes 417796
  21.2 14.0 %collective-permute-start.9 = (bf16[272,256]{1,0:T(8,128)(2,1)S(1)}, bf16[272,256]{1,0:T(8,128)(2,1)S(1)}, u32[]{:S(2)}, u32[]{:S(2)}) collective-permute-start(bf16[272,256]{1,0:T(8,128)(2,1)S(1)} %collective-permute-done.8.x), channel_id=1, source_target_pairs={{0,16},{16,0},{1,17},{17,1},{2,18},{18,2},{3,19},{19,3},{4,20},{20... | collective-permute-start | bytes 417800 | tf_op jit(solution)/shard_map/ppermute | solution.py:283
  21.3 11.1 %collective-permute-start.10 = (bf16[272,256]{1,0:T(8,128)(2,1)S(1)}, bf16[272,256]{1,0:T(8,128)(2,1)S(1)}, u32[]{:S(2)}, u32[]{:S(2)}) collective-permute-start(bf16[272,256]{1,0:T(8,128)(2,1)S(1)} %collective-permute-done.1.u2), channel_id=1, source_target_pairs={{0,16},{16,0},{1,17},{17,1},{2,18},{18,2},{3,19},{19,3},{4,20},{20... | collective-permute-start | bytes 417800 | tf_op jit(solution)/shard_map/ppermute | solution.py:283
  21.8 6.3 %collective-permute-start.2 = (bf16[272,256]{1,0:T(8,128)(2,1)S(1)}, bf16[272,256]{1,0:T(8,128)(2,1)S(1)}, u32[]{:S(2)}, u32[]{:S(2)}) collective-permute-start(bf16[272,256]{1,0:T(8,128)(2,1)S(1)} %collective-permute-done.1.u2), channel_id=1, source_target_pairs={{0,32},{32,64},{64,96},{96,128},{128,160},{160,192},{192,224},{224... | collective-permute-start | bytes 417800 | tf_op jit(solution)/shard_map/ppermute | solution.py:286
  24.7 7.7 %collective-permute-start.11 = (bf16[272,256]{1,0:T(8,128)(2,1)S(1)}, bf16[272,256]{1,0:T(8,128)(2,1)S(1)}, u32[]{:S(2)}, u32[]{:S(2)}) collective-permute-start(bf16[272,256]{1,0:T(8,128)(2,1)S(1)} %collective-permute-done.5.d2), channel_id=1, source_target_pairs={{0,16},{16,0},{1,17},{17,1},{2,18},{18,2},{3,19},{19,3},{4,20},{20... | collective-permute-start | bytes 417800 | tf_op jit(solution)/shard_map/ppermute | solution.py:283
  25.1 6.3 %collective-permute-start.6 = (bf16[272,256]{1,0:T(8,128)(2,1)S(1)}, bf16[272,256]{1,0:T(8,128)(2,1)S(1)}, u32[]{:S(2)}, u32[]{:S(2)}) collective-permute-start(bf16[272,256]{1,0:T(8,128)(2,1)S(1)} %collective-permute-done.5.d2), channel_id=1, source_target_pairs={{0,224},{32,0},{64,32},{96,64},{128,96},{160,128},{192,160},{224,1... | collective-permute-start | bytes 417800 | tf_op jit(solution)/shard_map/ppermute | solution.py:286
  28.1 7.1 %collective-permute-start.3 = (bf16[272,256]{1,0:T(8,128)(2,1)S(1)}, bf16[272,256]{1,0:T(8,128)(2,1)S(1)}, u32[]{:S(2)}, u32[]{:S(2)}) collective-permute-start(bf16[272,256]{1,0:T(8,128)(2,1)S(1)} %collective-permute-done.2.u3), channel_id=1, source_target_pairs={{0,16},{16,0},{1,17},{17,1},{2,18},{18,2},{3,19},{19,3},{4,20},{20... | collective-permute-start | bytes 417800 | tf_op jit(solution)/shard_map/ppermute | solution.py:283
  31.5 3.7 %collective-permute-start.7 = (bf16[272,256]{1,0:T(8,128)(2,1)S(1)}, bf16[272,256]{1,0:T(8,128)(2,1)S(1)}, u32[]{:S(2)}, u32[]{:S(2)}) collective-permute-start(bf16[272,256]{1,0:T(8,128)(2,1)S(1)} %collective-permute-done.6.d3), channel_id=1, source_target_pairs={{0,16},{16,0},{1,17},{17,1},{2,18},{18,2},{3,19},{19,3},{4,20},{20... | collective-permute-start | bytes 417800 | tf_op jit(solution)/shard_map/ppermute | solution.py:283
